TPU v7x, 32 devices: a whole 2x2x4 slice. The times are simulated.
32 devices in a mesh: wide: 8 (over z, x), narrow: 4 (over y, core).
Axes of the slice: x: 2, y: 2, z: 4, core: 2. Of those that a mesh axis runs over, the one named last changes fastest.
Arguments:
- embeddings: bfloat16 [8192, 512], P(('wide', 'narrow')), may hold values from -26 to 26
- partners: int32 [32, 7], P(('wide', 'narrow')), may hold values from -1 to 7, as said below
- pair_kind: int32 [32, 7], P(('wide', 'narrow')), may hold values from 0 to 1, as said below
- neighbors: int32 [7, 15, 8192], P(None, None, ('wide', 'narrow')), may hold values from 0 to 255
Outputs:
- gradient: float32 [8192, 512], P(('wide', 'narrow'))
- mean_loss: float32 [], replicated
Inputs may be any that keep to these rules, and one draw needn't show every extreme that they name: Row w * 4 + n lists the wide indices of that block's partners in ascending order, then -1 in the remaining slots; a partner has the same narrow index n, is never the block itself, appears once, and the pairing is mutual. In every narrow index one block is paired with all 7 others. `pair_kind`: 1 marks a graph pair, 0 a sampled negative or an empty slot; both directions of a pair carry the same mark, and every block has at least one graph pair.
All inputs are finite; a program needn't handle non-finite values.
Results may differ from a plain program's by a relative error of at most 0.0004.
Values may be sent and summed in bfloat16 or wider, within the bound.
No kernel may reach another device: no remote copies, remote signals or barrier semaphores. Data moves between devices by JAX's collectives and lax.ppermute only.
A program may use at most 64 MiB of HBM per device.

v0:
```python
import functools

import jax
import jax.numpy as jnp
from jax import lax
from jax.experimental import pallas as pl
from jax.experimental.pallas import tpu as pltpu
from jax.sharding import PartitionSpec as P


AXES = ("wide", "narrow")
VMEM = pl.BlockSpec(memory_space=pltpu.VMEM)
SMEM = pl.BlockSpec(memory_space=pltpu.SMEM)


def ring_position(index, groups):
    return jnp.where(index % 2 == 0, index // 2, groups - 1 - index // 2)


def ring_index(position, groups):
    return jnp.where(position < groups // 2, 2 * position, 2 * (groups - position) - 1)


def ring_order(groups):
    half = groups // 2
    return [2 * q if q < half else 2 * (groups - q) - 1 for q in range(groups)]


def shift_pairs(groups, offset):
    order = ring_order(groups)
    return [(order[q], order[(q + offset) % groups]) for q in range(groups)]


def ring_offsets(groups):
    half = groups // 2
    offsets = []
    for step in range(1, half):
        offsets += [step, -step]
    return offsets + [half]


def list_rows(knn):
    return (knn // 16 + 1) * 16


def tail_groups(groups):
    half = groups // 2
    return [(a, a + 1) for a in range(half - 3, 0, -2)]


def list_spot(groups, distance, block_rows, pad):
    half = groups // 2
    if distance >= half - 1:
        return 0, (distance - half + 1) * block_rows
    for group, (near, far) in enumerate(tail_groups(groups)):
        if distance in (near, far):
            return pad * (group + 1), (distance - near) * block_rows
    raise ValueError


def compiler_params(mib):
    return pltpu.CompilerParams(vmem_limit_bytes=mib << 20)


def cost(microseconds):
    return pl.CostEstimate(
        flops=int(microseconds * 8e8), bytes_accessed=int(microseconds * 2e6), transcendentals=0
    )


def prepare_body(groups, offsets, *refs):
    inputs, (right, left, own, facts) = refs[:3], refs[3:7]
    partners, marks, neighbors, sems = refs[7:]
    copies = [
        pltpu.make_async_copy(source, held, sems.at[k])
        for k, (source, held) in enumerate(zip(inputs, (partners, marks, neighbors)))
    ]
    for copy in copies:
        copy.start()
    for copy in copies:
        copy.wait()
    knn, block_rows = neighbors.shape[1:]
    pad = own.shape[1]
    half = groups // 2
    me = ring_position(lax.axis_index("wide"), groups)
    slots = partners.shape[1]
    marked_total = jnp.int32(0)
    present_total = jnp.int32(0)
    for place, offset in enumerate(offsets):
        target = ring_index(lax.rem(me + offset + groups, groups), groups)
        slot = jnp.int32(0)
        present = jnp.int32(0)
        marked = jnp.int32(0)
        for s in range(slots):
            hit = (partners[0, s] == target).astype(jnp.int32)
            slot += hit * s
            present += hit
            marked += hit * marks[0, s]
        marked_total += marked
        present_total += present
        rows = jnp.where(marked > 0, neighbors[slot], block_rows).astype(jnp.float32)
        flag = jnp.full((pad - knn, block_rows), present.astype(jnp.float32))
        entry = jnp.concatenate([rows, flag], axis=0).astype(jnp.bfloat16)
        own[place] = entry
        row, column = list_spot(groups, abs(offset), block_rows, pad)
        for message in (right, left) if offset == half else (right,) if offset > 0 else (left,):
            message[row : row + pad, column : column + block_rows] = entry
    facts[0, 0] = present_total
    facts[0, 1] = marked_total


def join_body(pad, right_block, left_block, right_lists, left_lists, right, left):
    block_rows = right_block.shape[0]
    for block, lists, out in ((right_block, right_lists, right), (left_block, left_lists, left)):
        out[0:pad, :] = lists[0:pad, :]
        out[pad : pad + block_rows, :] = block[...]
        kept = out.shape[0] - block_rows
        if kept > pad:
            out[pad + block_rows :, :] = lists[pad:kept, :]


def histogram(entry, knn, block_rows):
    width = 4 if knn < 16 else 8
    per = 32 // width
    shift = {4: 3, 8: 2}[width]
    value = entry.astype(jnp.float32).astype(jnp.int32)
    word = value >> shift
    bit = jnp.left_shift(jnp.int32(1), (value & (per - 1)) * width)
    words = block_rows // per
    index = lax.broadcasted_iota(jnp.int32, (words, block_rows), 0)
    total = jnp.zeros((words, block_rows), jnp.int32)
    for k in range(knn):
        total += jnp.where(word[k : k + 1, :] == index, bit[k : k + 1, :], 0)
    amount = (lax.broadcasted_iota(jnp.int32, (words, per, block_rows), 1)) * width
    spread = jnp.broadcast_to(total[:, None, :], (words, per, block_rows))
    counts = lax.shift_right_logical(spread, amount) & ((1 << width) - 1)
    return counts.reshape(block_rows, block_rows)


def own_counts_body(knn, own, out):
    block_rows = out.shape[1]
    for place in range(out.shape[0]):
        counts = histogram(own[place], knn, block_rows)
        out[place] = counts.astype(jnp.float32).astype(out.dtype)


def split(weight):
    high = weight.astype(jnp.bfloat16)
    return high, (weight - high.astype(jnp.float32)).astype(jnp.bfloat16)


NT = (((1,), (1,)), ((), ()))


def rows_of(refs, pieces):
    parts = [refs[k][a:b, :] for k, a, b in pieces]
    return parts[0] if len(parts) == 1 else jnp.concatenate(parts, axis=0)


def entry_of(refs, spot, pad, block_rows):
    k, row, column = spot
    return refs[k][row : row + pad, column : column + block_rows]


def norms_column(value, scale):
    wide = value.astype(jnp.float32)
    return jnp.sum(wide * wide, axis=1, keepdims=True) * scale


def norms_row(value, scale):
    wide = value.astype(jnp.float32)
    high, low = split(wide * wide)
    ones = jnp.ones((8, value.shape[1]), jnp.bfloat16)
    total = lax.dot_general(ones, high, NT, preferred_element_type=jnp.float32)
    total += lax.dot_general(ones, low, NT, preferred_element_type=jnp.float32)
    return total[0:1, :] * scale


def transposed(counts):
    rows = counts.shape[0]
    row = lax.broadcasted_iota(jnp.int32, (rows, rows), 0)
    column = lax.broadcasted_iota(jnp.int32, (rows, rows), 1)
    identity = jnp.where(row == column, 1.0, 0.0).astype(jnp.bfloat16)
    return lax.dot_general(identity, counts, NT, preferred_element_type=jnp.float32)


CHUNK = 32


def step_body(tiles, pairs, last_sums, constants, counted, first, *refs):
    features, knn, pad = constants
    facts, local_ref, own_ref = refs[:3]
    inputs = 3 if counted else 2
    tail = inputs + 1
    held_in = [] if first else refs[-tail - inputs : -tail]
    held = refs[-tail:-1]
    weights = refs[-1]
    sources = refs[3 : len(refs) - tail - (0 if first else inputs)]
    pulls, row_sums = held[:2]
    local = local_ref[...]
    block_rows = local.shape[0]
    scale = 1.0 / features
    local_norms = 1.0 + norms_column(local, scale)
    kernel_sum = jnp.zeros((8, block_rows), jnp.float32)
    attract_sum = jnp.zeros((8, block_rows), jnp.float32)

    def fold(value):
        return jnp.sum(value.reshape(CHUNK // 8, 8, block_rows), axis=0)

    for number, (place, pieces, spot) in enumerate(tiles):
        remote = rows_of(sources, pieces)
        entry = entry_of(sources, spot, pad, block_rows)
        back = histogram(entry, knn, block_rows).astype(jnp.float32)
        counts = transposed(own_ref[place]) + back
        present = entry.astype(jnp.float32)[knn : knn + 1, :]
        remote_norms = norms_row(remote, scale)
        inner = lax.dot_general(local, remote, NT, preferred_element_type=jnp.float32)
        for start in range(0, block_rows, CHUNK):
            rows = slice(start, start + CHUNK)
            ratio = local_norms[rows] + remote_norms - inner[rows] * (2.0 * scale)
            kernel = present / ratio
            near = counts[rows] * kernel
            far = kernel * kernel
            if counted:
                kernel_sum += fold(kernel)
                attract_sum += fold(counts[rows] * jnp.log(ratio))
            for k, weight in enumerate((near, far)):
                total = jnp.sum(weight, axis=1, keepdims=True)
                if number:
                    total += row_sums[k, rows, :]
                elif not first:
                    total += held_in[1][k, rows, :]
                row_sums[k, rows, :] = total
                high, low = split(weight)
                weights[2 * k, rows, :] = high
                weights[2 * k + 1, rows, :] = low
        for k in range(2):
            product = jnp.dot(weights[2 * k], remote, preferred_element_type=jnp.float32)
            product += jnp.dot(weights[2 * k + 1], remote, preferred_element_type=jnp.float32)
            if number:
                product += pulls[k]
            elif not first:
                product += held_in[0][k]
            pulls[k] = product
    for left_pieces, right_pieces, there, back_spot, weight in pairs:
        left, right = rows_of(sources, left_pieces), rows_of(sources, right_pieces)
        entry = entry_of(sources, there, pad, block_rows)
        forward = histogram(entry, knn, block_rows).astype(jnp.float32).astype(jnp.bfloat16)
        entry = entry_of(sources, back_spot, pad, block_rows)
        counts = transposed(forward) + histogram(entry, knn, block_rows).astype(jnp.float32)
        present = entry.astype(jnp.float32)[knn : knn + 1, :] * weight
        left_norms = 1.0 + norms_column(left, scale)
        right_norms = norms_row(right, scale)
        inner = lax.dot_general(left, right, NT, preferred_element_type=jnp.float32)
        for start in range(0, block_rows, CHUNK):
            rows = slice(start, start + CHUNK)
            ratio = left_norms[rows] + right_norms - inner[rows] * (2.0 * scale)
            kernel_sum += fold(present / ratio)
            attract_sum += fold((weight * counts[rows]) * jnp.log(ratio))
    if not counted:
        return
    if not first:
        kernel_sum += held_in[2][0]
        attract_sum += held_in[2][1]
    sums = held[2]
    if not last_sums:
        sums[0] = kernel_sum
        sums[1] = attract_sum
        return
    lane = lax.broadcasted_iota(jnp.int32, sums.shape, 1)
    values = (
        jnp.sum(kernel_sum),
        jnp.sum(attract_sum) * -0.5,
        facts[0, 1].astype(jnp.float32) * float(knn * block_rows),
        facts[0, 0].astype(jnp.float32) * float(block_rows * block_rows),
    )
    row = jnp.zeros(sums.shape, jnp.float32)
    for k, value in enumerate(values):
        row = jnp.where(lane == k, value, row)
    sums[...] = row


def finish_body(groups, features, table, center_ref, *refs):
    windows = refs[: len(table) - 1]
    local_ref, pulls, row_sums, gradient, loss, relative = refs[len(table) - 1 :]
    sources = (center_ref,) + windows
    for ref, rows in zip(sources, table):
        for row, offset in rows:
            relative[offset : offset + 1, :] = ref[row : row + 1, :]
    me = ring_position(lax.axis_index("wide"), groups)
    summed = jnp.sum(pltpu.roll(relative[...], me, 0), axis=0, keepdims=True)
    lane = lax.broadcasted_iota(jnp.int32, summed.shape, 1)

    def pick(k):
        return jnp.sum(jnp.where(lane == k, summed, 0.0), axis=1, keepdims=True)

    total, attract, edges, entries = pick(0), pick(1), pick(2), pick(3)
    loss[...] = -attract / edges + jnp.log(total / entries)
    repulsion = 2.0 * edges / total
    local = local_ref[...].astype(jnp.float32)
    rows = row_sums[0] - repulsion * row_sums[1]
    gradient[...] = (2.0 / features) * (rows * local - (pulls[0] - repulsion * pulls[1]))


def column_step(embeddings, partners, pair_kind, neighbors):
    block_rows, features = embeddings.shape
    knn = neighbors.shape[1]
    pad = list_rows(knn)
    groups = lax.axis_size("wide")
    half, quarter = groups // 2, groups // 4
    offsets = ring_offsets(groups)
    places = len(offsets)
    place_of = {offset: place for place, offset in enumerate(offsets)}
    tails = tail_groups(groups)
    list_height = pad * (len(tails) + 1)
    lists = jax.ShapeDtypeStruct((list_height, features), embeddings.dtype)

    def send(value, offset):
        return lax.ppermute(value, "wide", shift_pairs(groups, offset))

    def both(right, left):
        return [send(right, 1), send(left, -1)]

    def height(step):
        return pad * (1 + sum(far >= step for _, far in tails))

    blocks = both(embeddings, embeddings)
    right, left, own, facts = pl.pallas_call(
        functools.partial(prepare_body, groups, offsets),
        out_shape=[
            lists,
            lists,
            jax.ShapeDtypeStruct((places, pad, block_rows), jnp.bfloat16),
            jax.ShapeDtypeStruct((1, 2), jnp.int32),
        ],
        in_specs=[pl.BlockSpec(memory_space=pltpu.HBM)] * 3,
        out_specs=[VMEM, VMEM, VMEM, SMEM],
        scratch_shapes=[
            pltpu.SMEM(partners.shape, jnp.int32),
            pltpu.SMEM(pair_kind.shape, jnp.int32),
            pltpu.VMEM(neighbors.shape, jnp.int32),
            pltpu.SemaphoreType.DMA((3,)),
        ],
        compiler_params=compiler_params(8),
        cost_estimate=cost(1.5),
        name="prepare",
    )(*(pltpu.with_memory_space_constraint(x, pltpu.HBM) for x in (partners, pair_kind, neighbors)))
    notes = both(right, left)
    own_counts = pl.pallas_call(
        functools.partial(own_counts_body, knn),
        out_shape=jax.ShapeDtypeStruct((places, block_rows, block_rows), jnp.bfloat16),
        in_specs=[VMEM],
        out_specs=VMEM,
        compiler_params=compiler_params(8),
        cost_estimate=cost(1.0),
        name="own_counts",
    )(own)
    arrived = {1: blocks + notes}
    for step in range(2, quarter + 1):
        blocks = both(*blocks)
        notes = both(*(note[: height(step)] for note in notes))
        arrived[step] = blocks + notes
    message = jax.ShapeDtypeStruct((block_rows + height(quarter + 1), features), embeddings.dtype)
    right, left = pl.pallas_call(
        functools.partial(join_body, pad),
        out_shape=[message, message],
        in_specs=[VMEM] * 4,
        out_specs=[VMEM] * 2,
        compiler_params=compiler_params(4),
        cost_estimate=cost(0.3),
        name="join",
    )(*blocks, *notes)
    for step in range(quarter + 1, half):
        keep = block_rows + height(step)
        right, left = arrived[step] = both(right[:keep], left[:keep])
    middle = pad + block_rows // 2
    arrived[half] = both(right[:middle], left[middle : pad + block_rows])

    def spot_of(step, side, distance):
        row, column = list_spot(groups, distance, block_rows, pad)
        if step <= quarter:
            return side + 2, row, column
        return side, row + (block_rows if row else 0), column

    def block_of(step, side):
        start = 0 if step <= quarter else pad
        return [(side, start, start + block_rows)]

    state = None
    constants = (features, knn, pad)
    for step in range(1, half + 1):
        counted = step <= quarter
        sources = list(arrived[step])
        if step < half:
            tiles = [
                (place_of[-step], block_of(step, 0), spot_of(step, 0, step)),
                (place_of[step], block_of(step, 1), spot_of(step, 1, step)),
            ]
        else:
            pieces = [(0, pad, middle), (1, 0, block_rows // 2)]
            tiles = [(place_of[half], pieces, spot_of(step, 0, half))]
        pairs = []
        if step == quarter:
            for distance in range(quarter + 1, half + 1):
                lower = distance - quarter
                at, factor = 0, 1.0
                there = spot_of(step, 0, distance)
                if lower != quarter:
                    at, factor = len(sources), 2.0
                    sources += [arrived[lower][0], arrived[lower][2]]
                    there = (at + 1,) + there[1:]
                pairs.append(
                    (block_of(step, at), block_of(step, 1), there, spot_of(step, 1, distance), factor)
                )
        first = state is None
        operands = [facts, embeddings, own_counts] + sources
        shapes = [
            jax.ShapeDtypeStruct((2, block_rows, features), jnp.float32),
            jax.ShapeDtypeStruct((2, block_rows, 1), jnp.float32),
        ]
        if step == quarter:
            shapes.append(jax.ShapeDtypeStruct((1, 128), jnp.float32))
        elif counted:
            shapes.append(jax.ShapeDtypeStruct((2, 8, block_rows), jnp.float32))
        aliases = {}
        if not first:
            aliases = {len(operands) + k: k for k in range(2)}
            operands += state
        state = pl.pallas_call(
            functools.partial(step_body, tiles, pairs, step == quarter, constants, counted, first),
            out_shape=shapes,
            in_specs=[SMEM] + [VMEM] * (len(operands) - 1),
            out_specs=[VMEM] * len(shapes),
            scratch_shapes=[pltpu.VMEM((4, block_rows, block_rows), jnp.bfloat16)],
            input_output_aliases=aliases,
            compiler_params=compiler_params(12),
            cost_estimate=cost(1.0 * len(tiles) + 0.6 * len(pairs)),
        )(*operands)
        if step == quarter:
            window, *_ = state[2:]
            state = state[:2]
    columns = lax.axis_size("narrow")
    bit = 1
    while bit < columns:
        other = lax.ppermute(window, "narrow", [(k, k ^ bit) for k in range(columns)])
        window = window + other
        bit *= 2
    reach, received = 0, []
    table = [[(0, 0)]]
    while 2 * reach + 1 < groups:
        if reach:
            window = jnp.concatenate([received[1], window, received[0]], axis=0)
            table = [[(row, (row - reach) % groups) for row in range(2 * reach + 1)]]
        stride = 2 * reach + 1
        received = [send(window, -stride), send(window, stride)]
        seen = {offset for _, offset in table[0]}
        for sign in (1, -1):
            rows = []
            for row in range(2 * reach + 1):
                offset = (sign * stride + row - reach) % groups
                if offset not in seen:
                    seen.add(offset)
                    rows.append((row, offset))
            table.append(rows)
        reach = 3 * reach + 1
    gradient, loss = pl.pallas_call(
        functools.partial(finish_body, groups, features, table),
        out_shape=[
            jax.ShapeDtypeStruct((block_rows, features), jnp.float32),
            jax.ShapeDtypeStruct((1, 1), jnp.float32),
        ],
        in_specs=[VMEM] * (3 + len(table)),
        out_specs=[VMEM] * 2,
        scratch_shapes=[pltpu.VMEM((groups, 128), jnp.float32)],
        compiler_params=compiler_params(12),
        cost_estimate=cost(1.0),
        name="finish",
    )(window, *received, embeddings, *state)
    return gradient, loss.reshape(())


def solution(mesh):
    in_specs = (P(AXES, None), P(AXES, None), P(AXES, None), P(None, None, AXES))
    return jax.shard_map(
        column_step, mesh=mesh, in_specs=in_specs, out_specs=(P(AXES, None), P()), check_vma=False
    )
```

profile of v0, /device:TPU:0, one launch (start us, length us, event | category | flops | bytes accessed | tf_op | source)
XLA Modules:
  0.0 52.3 jit_solution(3971821566109022212)
XLA Ops:
  0.6 3.1 %collective-permute-start = (bf16[256,512]{1,0:T(8,128)(2,1)}, bf16[256,512]{1,0:T(8,128)(2,1)S(1)}, u32[]{:S(2)}, u32[]{:S(2)}) collective-permute-start(bf16[256,512]{1,0:T(8,128)(2,1)} %refs_2_.3), channel_id=1, source_target_pairs={{0,8},{8,16},{16,24},{24,28},{28,20},{20,12},{12,4},{4,0},{1,9},{9... | collective-permute-start | bytes 786440 | tf_op jit(solution)/shard_map/ppermute | solution.py:319
  3.7 0.0 collective-permute-start.2
  3.7 6.4 %collective-permute-done.refs_3_.refs_7_ = bf16[256,512]{1,0:T(8,128)(2,1)S(1)} collective-permute-done((bf16[256,512]{1,0:T(8,128)(2,1)}, bf16[256,512]{1,0:T(8,128)(2,1)S(1)}, u32[]{:S(2)}, u32[]{:S(2)}) %collective-permute-start) | collective-permute-done | bytes 262176 | tf_op jit(solution)/shard_map/ppermute | solution.py:319
  10.2 1.8 %collective-permute-start.1 = (bf16[256,512]{1,0:T(8,128)(2,1)S(1)}, bf16[256,512]{1,0:T(8,128)(2,1)S(1)}, u32[]{:S(2)}, u32[]{:S(2)}) collective-permute-start(bf16[256,512]{1,0:T(8,128)(2,1)S(1)} %collective-permute-done.refs_3_.refs_7_), channel_id=1, source_target_pairs={{0,8},{8,16},{16,24},{24,28},{28,20},{20,12},{12,4},{4,0},{1,9},{9... | collective-permute-start | bytes 786440 | tf_op jit(solution)/shard_map/ppermute | solution.py:319
  12.0 0.0 collective-permute-done.2.refs_4_
  12.0 0.2 collective-permute-start.3
  12.2 1.6 %prepare.1 = (bf16[32,512]{1,0:T(8,128)(2,1)S(1)}, bf16[32,512]{1,0:T(8,128)(2,1)S(1)}, bf16[7,16,256]{2,1,0:T(8,128)(2,1)S(1)}, s32[1,2]{1,0:T(1,128)S(1)}) custom-call(s32[1,7]{1,0:T(1,128)} %refs_0_.1, s32[1,7]{1,0:T(1,128)} %refs_1_.5, s32[7,15,256]{2,1,0:T(8,128)} %refs_2_.2), custom_call_target="tpu_custom_call" | custom-call | flops 1200000000 | bytes 3000000 | tf_op jit(solution)/shard_map/prepare/pallas_call | solution.py:328
  13.8 1.9 %collective-permute-start.4 = (bf16[32,512]{1,0:T(8,128)(2,1)S(1)}, bf16[32,512]{1,0:T(8,128)(2,1)S(1)}, u32[]{:S(2)}, u32[]{:S(2)}) collective-permute-start(bf16[32,512]{1,0:T(8,128)(2,1)S(1)} %get-tuple-element.22), channel_id=1, source_target_pairs={{0,8},{8,16},{16,24},{24,28},{28,20},{20,12},{12,4},{4,0},{1,9},{9... | collective-permute-start | bytes 98312 | tf_op jit(solution)/shard_map/ppermute | solution.py:319
  15.7 0.2 collective-permute-start.6
  15.9 0.0 copy-start
  15.9 0.9 %own_counts.1.refs_2_ = bf16[7,256,256]{2,1,0:T(8,128)(2,1)S(1)} custom-call(bf16[7,16,256]{2,1,0:T(8,128)(2,1)S(1)} %get-tuple-element.21.own), custom_call_target="tpu_custom_call" | custom-call | flops 800000000 | bytes 2000000 | tf_op jit(solution)/shard_map/own_counts/pallas_call | solution.py:349
  16.8 1.5 %collective-permute-done.4.refs_5_.refs_8_ = bf16[32,512]{1,0:T(8,128)(2,1)S(1)} collective-permute-done((bf16[32,512]{1,0:T(8,128)(2,1)S(1)}, bf16[32,512]{1,0:T(8,128)(2,1)S(1)}, u32[]{:S(2)}, u32[]{:S(2)}) %collective-permute-start.4) | collective-permute-done | bytes 32800 | tf_op jit(solution)/shard_map/ppermute | solution.py:319
  18.3 1.5 %collective-permute-start.5 = (bf16[32,512]{1,0:T(8,128)(2,1)S(1)}, bf16[32,512]{1,0:T(8,128)(2,1)S(1)}, u32[]{:S(2)}, u32[]{:S(2)}) collective-permute-start(bf16[32,512]{1,0:T(8,128)(2,1)S(1)} %collective-permute-done.4.refs_5_.refs_8_), channel_id=1, source_target_pairs={{0,8},{8,16},{16,24},{24,28},{28,20},{20,12},{12,4},{4,0},{1,9},{9... | collective-permute-start | bytes 98312 | tf_op jit(solution)/shard_map/ppermute | solution.py:319
  19.9 0.0 collective-permute-done.6.refs_6_
  19.9 0.5 collective-permute-start.7
  20.4 0.0 copy-done
  20.4 2.1 %shard_map.59 = (f32[2,256,512]{2,1,0:T(8,128)S(1)}, f32[2,256,1]{2,1,0:T(8,128)S(1)}, f32[2,8,256]{2,1,0:T(8,128)S(1)}) custom-call(s32[1,2]{1,0:T(1,128)S(1)} %get-tuple-element.20.refs_0_, bf16[256,512]{1,0:T(8,128)(2,1)S(1)} %copy-done, bf16[7,256,256]{2,1,0:T(8,128)(2,1)S(1)} %own_counts.1.refs_2_, ...), custom_call_target="tpu_custom_call" | custom-call | flops 1600000000 | bytes 4000000 | tf_op jit(solution)/shard_map/pallas_call | solution.py:429
  22.5 0.0 collective-permute-done.5.refs_5_.right_lists
  22.5 1.3 %collective-permute-done.7.refs_6_.left_lists = bf16[32,512]{1,0:T(8,128)(2,1)S(1)} collective-permute-done((bf16[32,512]{1,0:T(8,128)(2,1)S(1)}, bf16[32,512]{1,0:T(8,128)(2,1)S(1)}, u32[]{:S(2)}, u32[]{:S(2)}) %collective-permute-start.7) | collective-permute-done | bytes 32800 | tf_op jit(solution)/shard_map/ppermute | solution.py:319
  23.8 0.0 collective-permute-done.1.refs_3_.right_block
  23.8 0.0 collective-permute-done.3.refs_4_.left_block
  23.9 1.6 %collective-permute-start.14 = (bf16[272,512]{1,0:T(8,128)(2,1)S(1)}, bf16[272,512]{1,0:T(8,128)(2,1)S(1)}, u32[]{:S(2)}, u32[]{:S(2)}) collective-permute-start(bf16[272,512]{1,0:T(8,128)(2,1)S(1)} %get-tuple-element.28), channel_id=1, source_target_pairs={{0,8},{8,16},{16,24},{24,28},{28,20},{20,12},{12,4},{4,0},{1,9},{9... | collective-permute-start | bytes 835592 | tf_op jit(solution)/shard_map/ppermute | solution.py:319
  25.5 0.4 collective-permute-start.16
  25.9 3.2 %shard_map.60 = (f32[2,256,512]{2,1,0:T(8,128)S(1)}, f32[2,256,1]{2,1,0:T(8,128)S(1)}, f32[1,128]{1,0:T(1,128)S(1)}) custom-call(s32[1,2]{1,0:T(1,128)S(1)} %get-tuple-element.20.refs_0_, bf16[256,512]{1,0:T(8,128)(2,1)S(1)} %copy-done, bf16[7,256,256]{2,1,0:T(8,128)(2,1)S(1)} %own_counts.1.refs_2_, ...), custom_call_target="tpu_custom_call", output_to_operand_aliasing={{0}: (9, {}), {1}: (10, {})} | custom-call | flops 2560000000 | bytes 6400000 | tf_op jit(solution)/shard_map/pallas_call | solution.py:429
  29.1 0.1 collective-permute-start.8
  29.2 1.1 %collective-permute-done.8 = f32[1,128]{1,0:T(1,128)S(1)} collective-permute-done((f32[1,128]{1,0:T(1,128)S(1)}, f32[1,128]{1,0:T(1,128)S(1)}, u32[]{:S(2)}, u32[]{:S(2)}) %collective-permute-start.8) | collective-permute-done | bytes 544 | tf_op jit(solution)/shard_map/ppermute | solution.py:445
  30.3 1.5 %collective-permute-start.9 = (f32[1,128]{1,0:T(1,128)S(1)}, f32[1,128]{1,0:T(1,128)S(1)}, u32[]{:S(2)}, u32[]{:S(2)}) collective-permute-start(f32[1,128]{1,0:T(1,128)S(1)} %add.6), channel_id=1, source_target_pairs={{0,2},{1,3},{2,0},{3,1},{4,6},{5,7},{6,4},{7,5},{8,10},{9,11},{10,... | collective-permute-start | bytes 1544 | tf_op jit(solution)/shard_map/ppermute | solution.py:445
  31.8 2.1 %collective-permute-done.9 = f32[1,128]{1,0:T(1,128)S(1)} collective-permute-done((f32[1,128]{1,0:T(1,128)S(1)}, f32[1,128]{1,0:T(1,128)S(1)}, u32[]{:S(2)}, u32[]{:S(2)}) %collective-permute-start.9) | collective-permute-done | bytes 544 | tf_op jit(solution)/shard_map/ppermute | solution.py:445
  33.9 1.6 %collective-permute-start.10 = (f32[1,128]{1,0:T(1,128)S(1)}, f32[1,128]{1,0:T(1,128)S(1)}, u32[]{:S(2)}, u32[]{:S(2)}) collective-permute-start(f32[1,128]{1,0:T(1,128)S(1)} %add.7), channel_id=1, source_target_pairs={{0,8},{8,16},{16,24},{24,28},{28,20},{20,12},{12,4},{4,0},{1,9},{9... | collective-permute-start | bytes 1544 | tf_op jit(solution)/shard_map/ppermute | solution.py:319
  35.5 0.4 collective-permute-start.11
  35.9 1.5 %collective-permute-done.10 = f32[1,128]{1,0:T(1,128)S(1)} collective-permute-done((f32[1,128]{1,0:T(1,128)S(1)}, f32[1,128]{1,0:T(1,128)S(1)}, u32[]{:S(2)}, u32[]{:S(2)}) %collective-permute-start.10) | collective-permute-done | bytes 544 | tf_op jit(solution)/shard_map/ppermute | solution.py:319
  37.5 1.6 %collective-permute-done.11 = f32[1,128]{1,0:T(1,128)S(1)} collective-permute-done((f32[1,128]{1,0:T(1,128)S(1)}, f32[1,128]{1,0:T(1,128)S(1)}, u32[]{:S(2)}, u32[]{:S(2)}) %collective-permute-start.11) | collective-permute-done | bytes 544 | tf_op jit(solution)/shard_map/ppermute | solution.py:319
  39.1 1.3 %collective-permute-start.12 = (f32[3,128]{1,0:T(4,128)S(1)}, f32[3,128]{1,0:T(4,128)S(1)}, u32[]{:S(2)}, u32[]{:S(2)}) collective-permute-start(f32[3,128]{1,0:T(4,128)S(1)} %pad_maximum_fusion.center_ref), channel_id=1, source_target_pairs={{0,20},{8,12},{16,4},{24,0},{28,8},{20,16},{12,24},{4,28},{1,21},{... | collective-permute-start | bytes 4616 | tf_op jit(solution)/shard_map/ppermute | solution.py:319
  40.4 2.6 %collective-permute-start.13 = (f32[3,128]{1,0:T(4,128)S(1)}, f32[3,128]{1,0:T(4,128)S(1)}, u32[]{:S(2)}, u32[]{:S(2)}) collective-permute-start(f32[3,128]{1,0:T(4,128)S(1)} %pad_maximum_fusion.center_ref), channel_id=1, source_target_pairs={{0,24},{8,28},{16,20},{24,12},{28,4},{20,0},{12,8},{4,16},{1,25},{... | collective-permute-start | bytes 4616 | tf_op jit(solution)/shard_map/ppermute | solution.py:319
  42.9 0.0 collective-permute-done.14.refs_3_
  43.0 1.6 %collective-permute-start.15 = (bf16[144,512]{1,0:T(8,128)(2,1)S(1)}, bf16[144,512]{1,0:T(8,128)(2,1)S(1)}, u32[]{:S(2)}, u32[]{:S(2)}) collective-permute-start(bf16[144,512]{1,0:T(8,128)(2,1)S(1)} %slice.8), channel_id=1, source_target_pairs={{0,8},{8,16},{16,24},{24,28},{28,20},{20,12},{12,4},{4,0},{1,9},{9... | collective-permute-start | bytes 442376 | tf_op jit(solution)/shard_map/ppermute | solution.py:319
  44.6 0.0 collective-permute-done.16.refs_4_
  44.6 0.5 collective-permute-start.17
  45.1 2.2 %shard_map.61 = (f32[2,256,512]{2,1,0:T(8,128)S(1)}, f32[2,256,1]{2,1,0:T(8,128)S(1)}) custom-call(s32[1,2]{1,0:T(1,128)S(1)} %get-tuple-element.20.refs_0_, bf16[256,512]{1,0:T(8,128)(2,1)S(1)} %copy-done, bf16[7,256,256]{2,1,0:T(8,128)(2,1)S(1)} %own_counts.1.refs_2_, ...), custom_call_target="tpu_custom_call", output_to_operand_aliasing={{0}: (5, {}), {1}: (6, {})} | custom-call | flops 1600000000 | bytes 4000000 | tf_op jit(solution)/shard_map/pallas_call | solution.py:429
  47.3 2.3 %collective-permute-done.17.refs_4_ = bf16[128,512]{1,0:T(8,128)(2,1)S(1)} collective-permute-done((bf16[128,512]{1,0:T(8,128)(2,1)S(1)}, bf16[128,512]{1,0:T(8,128)(2,1)S(1)}, u32[]{:S(2)}, u32[]{:S(2)}) %collective-permute-start.17) | collective-permute-done | bytes 131104 | tf_op jit(solution)/shard_map/ppermute | solution.py:319
  49.6 0.0 collective-permute-done.15.refs_3_
  49.6 1.6 %shard_map.62 = (f32[2,256,512]{2,1,0:T(8,128)S(1)}, f32[2,256,1]{2,1,0:T(8,128)S(1)}) custom-call(s32[1,2]{1,0:T(1,128)S(1)} %get-tuple-element.20.refs_0_, bf16[256,512]{1,0:T(8,128)(2,1)S(1)} %copy-done, bf16[7,256,256]{2,1,0:T(8,128)(2,1)S(1)} %own_counts.1.refs_2_, ...), custom_call_target="tpu_custom_call", output_to_operand_aliasing={{0}: (5, {}), {1}: (6, {})} | custom-call | flops 800000000 | bytes 2000000 | tf_op jit(solution)/shard_map/pallas_call | solution.py:429
  51.2 0.0 collective-permute-done.12.refs_0_
  51.2 0.0 collective-permute-done.13.refs_1_
  51.2 1.1 %finish.1 = (f32[256,512]{1,0:T(8,128)}, f32[1,1]{1,0:T(1,128)}) custom-call(f32[3,128]{1,0:T(4,128)S(1)} %pad_maximum_fusion.center_ref, f32[3,128]{1,0:T(4,128)S(1)} %collective-permute-done.12.refs_0_, f32[3,128]{1,0:T(4,128)S(1)} %collective-permute-done.13.refs_1_, bf16[256,512]{1,0:T(8,128)(2,1)S(1)} %copy-done, ...), custom_call_target="tpu_custom_call" | custom-call | flops 800000000 | bytes 2000000 | tf_op jit(solution)/shard_map/finish/pallas_call | solution.py:466
  (6 shorter events, 0.1 us)
Async XLA Ops:
  0.6 9.5 %collective-permute-start = (bf16[256,512]{1,0:T(8,128)(2,1)}, bf16[256,512]{1,0:T(8,128)(2,1)S(1)}, u32[]{:S(2)}, u32[]{:S(2)}) collective-permute-start(bf16[256,512]{1,0:T(8,128)(2,1)} %refs_2_.3), channel_id=1, source_target_pairs={{0,8},{8,16},{16,24},{24,28},{28,20},{20,12},{12,4},{4,0},{1,9},{9... | collective-permute-start | bytes 786440 | tf_op jit(solution)/shard_map/ppermute | solution.py:319
  3.7 8.3 %collective-permute-start.2 = (bf16[256,512]{1,0:T(8,128)(2,1)}, bf16[256,512]{1,0:T(8,128)(2,1)S(1)}, u32[]{:S(2)}, u32[]{:S(2)}) collective-permute-start(bf16[256,512]{1,0:T(8,128)(2,1)} %refs_2_.3), channel_id=1, source_target_pairs={{0,4},{8,0},{16,8},{24,16},{28,24},{20,28},{12,20},{4,12},{1,5},{9... | collective-permute-start | bytes 786440 | tf_op jit(solution)/shard_map/ppermute | solution.py:319
  10.2 13.6 %collective-permute-start.1 = (bf16[256,512]{1,0:T(8,128)(2,1)S(1)}, bf16[256,512]{1,0:T(8,128)(2,1)S(1)}, u32[]{:S(2)}, u32[]{:S(2)}) collective-permute-start(bf16[256,512]{1,0:T(8,128)(2,1)S(1)} %collective-permute-done.refs_3_.refs_7_), channel_id=1, source_target_pairs={{0,8},{8,16},{16,24},{24,28},{28,20},{20,12},{12,4},{4,0},{1,9},{9... | collective-permute-start | bytes 786440 | tf_op jit(solution)/shard_map/ppermute | solution.py:319
  12.0 11.8 %collective-permute-start.3 = (bf16[256,512]{1,0:T(8,128)(2,1)S(1)}, bf16[256,512]{1,0:T(8,128)(2,1)S(1)}, u32[]{:S(2)}, u32[]{:S(2)}) collective-permute-start(bf16[256,512]{1,0:T(8,128)(2,1)S(1)} %collective-permute-done.2.refs_4_), channel_id=1, source_target_pairs={{0,4},{8,0},{16,8},{24,16},{28,24},{20,28},{12,20},{4,12},{1,5},{9... | collective-permute-start | bytes 786440 | tf_op jit(solution)/shard_map/ppermute | solution.py:319
  13.8 4.5 %collective-permute-start.4 = (bf16[32,512]{1,0:T(8,128)(2,1)S(1)}, bf16[32,512]{1,0:T(8,128)(2,1)S(1)}, u32[]{:S(2)}, u32[]{:S(2)}) collective-permute-start(bf16[32,512]{1,0:T(8,128)(2,1)S(1)} %get-tuple-element.22), channel_id=1, source_target_pairs={{0,8},{8,16},{16,24},{24,28},{28,20},{20,12},{12,4},{4,0},{1,9},{9... | collective-permute-start | bytes 98312 | tf_op jit(solution)/shard_map/ppermute | solution.py:319
  15.7 4.2 %collective-permute-start.6 = (bf16[32,512]{1,0:T(8,128)(2,1)S(1)}, bf16[32,512]{1,0:T(8,128)(2,1)S(1)}, u32[]{:S(2)}, u32[]{:S(2)}) collective-permute-start(bf16[32,512]{1,0:T(8,128)(2,1)S(1)} %get-tuple-element.23), channel_id=1, source_target_pairs={{0,4},{8,0},{16,8},{24,16},{28,24},{20,28},{12,20},{4,12},{1,5},{9... | collective-permute-start | bytes 98312 | tf_op jit(solution)/shard_map/ppermute | solution.py:319
  15.9 4.5 %copy-start = (bf16[256,512]{1,0:T(8,128)(2,1)S(1)}, bf16[256,512]{1,0:T(8,128)(2,1)}, u32[]{:S(2)}) copy-start(bf16[256,512]{1,0:T(8,128)(2,1)} %refs_2_.3) | copy-start | bytes 786436
  18.3 4.2 %collective-permute-start.5 = (bf16[32,512]{1,0:T(8,128)(2,1)S(1)}, bf16[32,512]{1,0:T(8,128)(2,1)S(1)}, u32[]{:S(2)}, u32[]{:S(2)}) collective-permute-start(bf16[32,512]{1,0:T(8,128)(2,1)S(1)} %collective-permute-done.4.refs_5_.refs_8_), channel_id=1, source_target_pairs={{0,8},{8,16},{16,24},{24,28},{28,20},{20,12},{12,4},{4,0},{1,9},{9... | collective-permute-start | bytes 98312 | tf_op jit(solution)/shard_map/ppermute | solution.py:319
  19.9 3.9 %collective-permute-start.7 = (bf16[32,512]{1,0:T(8,128)(2,1)S(1)}, bf16[32,512]{1,0:T(8,128)(2,1)S(1)}, u32[]{:S(2)}, u32[]{:S(2)}) collective-permute-start(bf16[32,512]{1,0:T(8,128)(2,1)S(1)} %collective-permute-done.6.refs_6_), channel_id=1, source_target_pairs={{0,4},{8,0},{16,8},{24,16},{28,24},{20,28},{12,20},{4,12},{1,5},{9... | collective-permute-start | bytes 98312 | tf_op jit(solution)/shard_map/ppermute | solution.py:319
  23.9 19.1 %collective-permute-start.14 = (bf16[272,512]{1,0:T(8,128)(2,1)S(1)}, bf16[272,512]{1,0:T(8,128)(2,1)S(1)}, u32[]{:S(2)}, u32[]{:S(2)}) collective-permute-start(bf16[272,512]{1,0:T(8,128)(2,1)S(1)} %get-tuple-element.28), channel_id=1, source_target_pairs={{0,8},{8,16},{16,24},{24,28},{28,20},{20,12},{12,4},{4,0},{1,9},{9... | collective-permute-start | bytes 835592 | tf_op jit(solution)/shard_map/ppermute | solution.py:319
  25.5 19.1 %collective-permute-start.16 = (bf16[272,512]{1,0:T(8,128)(2,1)S(1)}, bf16[272,512]{1,0:T(8,128)(2,1)S(1)}, u32[]{:S(2)}, u32[]{:S(2)}) collective-permute-start(bf16[272,512]{1,0:T(8,128)(2,1)S(1)} %get-tuple-element.29), channel_id=1, source_target_pairs={{0,4},{8,0},{16,8},{24,16},{28,24},{20,28},{12,20},{4,12},{1,5},{9... | collective-permute-start | bytes 835592 | tf_op jit(solution)/shard_map/ppermute | solution.py:319
  29.1 1.2 %collective-permute-start.8 = (f32[1,128]{1,0:T(1,128)S(1)}, f32[1,128]{1,0:T(1,128)S(1)}, u32[]{:S(2)}, u32[]{:S(2)}) collective-permute-start(f32[1,128]{1,0:T(1,128)S(1)} %get-tuple-element.27), channel_id=1, source_target_pairs={{0,1},{1,0},{2,3},{3,2},{4,5},{5,4},{6,7},{7,6},{8,9},{9,8},{10,11... | collective-permute-start | bytes 1544 | tf_op jit(solution)/shard_map/ppermute | solution.py:445
  30.3 3.6 %collective-permute-start.9 = (f32[1,128]{1,0:T(1,128)S(1)}, f32[1,128]{1,0:T(1,128)S(1)}, u32[]{:S(2)}, u32[]{:S(2)}) collective-permute-start(f32[1,128]{1,0:T(1,128)S(1)} %add.6), channel_id=1, source_target_pairs={{0,2},{1,3},{2,0},{3,1},{4,6},{5,7},{6,4},{7,5},{8,10},{9,11},{10,... | collective-permute-start | bytes 1544 | tf_op jit(solution)/shard_map/ppermute | solution.py:445
  33.9 3.6 %collective-permute-start.10 = (f32[1,128]{1,0:T(1,128)S(1)}, f32[1,128]{1,0:T(1,128)S(1)}, u32[]{:S(2)}, u32[]{:S(2)}) collective-permute-start(f32[1,128]{1,0:T(1,128)S(1)} %add.7), channel_id=1, source_target_pairs={{0,8},{8,16},{16,24},{24,28},{28,20},{20,12},{12,4},{4,0},{1,9},{9... | collective-permute-start | bytes 1544 | tf_op jit(solution)/shard_map/ppermute | solution.py:319
  35.5 3.6 %collective-permute-start.11 = (f32[1,128]{1,0:T(1,128)S(1)}, f32[1,128]{1,0:T(1,128)S(1)}, u32[]{:S(2)}, u32[]{:S(2)}) collective-permute-start(f32[1,128]{1,0:T(1,128)S(1)} %add.7), channel_id=1, source_target_pairs={{0,4},{8,0},{16,8},{24,16},{28,24},{20,28},{12,20},{4,12},{1,5},{9... | collective-permute-start | bytes 1544 | tf_op jit(solution)/shard_map/ppermute | solution.py:319
  39.1 12.1 %collective-permute-start.12 = (f32[3,128]{1,0:T(4,128)S(1)}, f32[3,128]{1,0:T(4,128)S(1)}, u32[]{:S(2)}, u32[]{:S(2)}) collective-permute-start(f32[3,128]{1,0:T(4,128)S(1)} %pad_maximum_fusion.center_ref), channel_id=1, source_target_pairs={{0,20},{8,12},{16,4},{24,0},{28,8},{20,16},{12,24},{4,28},{1,21},{... | collective-permute-start | bytes 4616 | tf_op jit(solution)/shard_map/ppermute | solution.py:319
  40.4 10.8 %collective-permute-start.13 = (f32[3,128]{1,0:T(4,128)S(1)}, f32[3,128]{1,0:T(4,128)S(1)}, u32[]{:S(2)}, u32[]{:S(2)}) collective-permute-start(f32[3,128]{1,0:T(4,128)S(1)} %pad_maximum_fusion.center_ref), channel_id=1, source_target_pairs={{0,24},{8,28},{16,20},{24,12},{28,4},{20,0},{12,8},{4,16},{1,25},{... | collective-permute-start | bytes 4616 | tf_op jit(solution)/shard_map/ppermute | solution.py:319
  43.0 6.7 %collective-permute-start.15 = (bf16[144,512]{1,0:T(8,128)(2,1)S(1)}, bf16[144,512]{1,0:T(8,128)(2,1)S(1)}, u32[]{:S(2)}, u32[]{:S(2)}) collective-permute-start(bf16[144,512]{1,0:T(8,128)(2,1)S(1)} %slice.8), channel_id=1, source_target_pairs={{0,8},{8,16},{16,24},{24,28},{28,20},{20,12},{12,4},{4,0},{1,9},{9... | collective-permute-start | bytes 442376 | tf_op jit(solution)/shard_map/ppermute | solution.py:319
  44.6 5.0 %collective-permute-start.17 = (bf16[128,512]{1,0:T(8,128)(2,1)S(1)}, bf16[128,512]{1,0:T(8,128)(2,1)S(1)}, u32[]{:S(2)}, u32[]{:S(2)}) collective-permute-start(bf16[128,512]{1,0:T(8,128)(2,1)S(1)} %slice.9), channel_id=1, source_target_pairs={{0,4},{8,0},{16,8},{24,16},{28,24},{20,28},{12,20},{4,12},{1,5},{9... | collective-permute-start | bytes 393224 | tf_op jit(solution)/shard_map/ppermute | solution.py:319
where the time goes:
time: 52.5 us; the launch traced here: 52.3 us
  starting transfers between devices  20.9 us (40%)
  waiting for transfers between devices  17.9 us (34%)
  Pallas kernels  12.7 us (24%)
  between operations  0.74 us (1%)
    ppermute x16, starting transfers between devices, send(): return lax.ppermute(value, 'wide', shift_pairs(groups, offset))  19.3 us
    ppermute x16, waiting for transfers between devices, send(): return lax.ppermute(value, 'wide', shift_pairs(groups, offset))  14.7 us
    pallas_call x4, Pallas kernels, column_step(): pl.pallas_call(functools.partial(step_body, tiles, pairs, step == quarter...  9.09 us
    ppermute x2, waiting for transfers between devices, column_step(): lax.ppermute(window, 'narrow', [(k, k ^ bit) for k in range(columns)])  3.21 us
    pallas_call x1, Pallas kernels, column_step(): pl.pallas_call(functools.partial(prepare_body, groups, offsets), out_shap...  1.63 us
    ppermute x2, starting transfers between devices, column_step(): lax.ppermute(window, 'narrow', [(k, k ^ bit) for k in range(columns)])  1.58 us
    pallas_call x1, Pallas kernels, column_step(): pl.pallas_call(functools.partial(finish_body, groups, features, table), o...  1.08 us
  transfers between devices with their start and end apart: 18, of which 8 were waited for; matrix products, arithmetic and copies ran while one was open for 0% of the time, Pallas kernels for 22%

commit v1 on v0

v1 whole, which is shorter than its diff:
```python
import functools

import jax
import jax.numpy as jnp
from jax import lax
from jax.experimental import pallas as pl
from jax.experimental.pallas import tpu as pltpu
from jax.sharding import PartitionSpec as P


AXES = ("wide", "narrow")
VMEM = pl.BlockSpec(memory_space=pltpu.VMEM)
SMEM = pl.BlockSpec(memory_space=pltpu.SMEM)


def ring_position(index, groups):
    return jnp.where(index % 2 == 0, index // 2, groups - 1 - index // 2)


def ring_index(position, groups):
    return jnp.where(position < groups // 2, 2 * position, 2 * (groups - position) - 1)


def ring_order(groups):
    half = groups // 2
    return [2 * q if q < half else 2 * (groups - q) - 1 for q in range(groups)]


def shift_pairs(groups, offset):
    order = ring_order(groups)
    return [(order[q], order[(q + offset) % groups]) for q in range(groups)]


def ring_offsets(groups):
    half = groups // 2
    offsets = []
    for step in range(1, half):
        offsets += [step, -step]
    return offsets + [half]


def list_rows(knn):
    return (knn // 16 + 1) * 16


def tail_groups(groups):
    half = groups // 2
    return [(a, a + 1) for a in range(half - 3, 0, -2)]


def list_spot(groups, distance, block_rows, pad):
    half = groups // 2
    if distance >= half - 1:
        return 0, (distance - half + 1) * block_rows
    for group, (near, far) in enumerate(tail_groups(groups)):
        if distance in (near, far):
            return pad * (group + 1), (distance - near) * block_rows
    raise ValueError


def compiler_params(mib):
    return pltpu.CompilerParams(vmem_limit_bytes=mib << 20)


def cost(microseconds):
    return pl.CostEstimate(
        flops=int(microseconds * 8e8), bytes_accessed=int(microseconds * 2e6), transcendentals=0
    )


def prepare_body(groups, offsets, *refs):
    inputs, (right, left, own, base, local) = refs[:4], refs[4:9]
    partners, marks, neighbors, sems = refs[9:]
    copies = [
        pltpu.make_async_copy(source, held, sems.at[k])
        for k, (source, held) in enumerate(zip(inputs, (partners, marks, neighbors, local)))
    ]
    for copy in copies:
        copy.start()
    for copy in copies[:3]:
        copy.wait()
    knn, block_rows = neighbors.shape[1:]
    pad = own.shape[1]
    half = groups // 2
    me = ring_position(lax.axis_index("wide"), groups)
    slots = partners.shape[1]
    marked_total = jnp.int32(0)
    present_total = jnp.int32(0)
    for place, offset in enumerate(offsets):
        target = ring_index(lax.rem(me + offset + groups, groups), groups)
        slot = jnp.int32(0)
        present = jnp.int32(0)
        marked = jnp.int32(0)
        for s in range(slots):
            hit = (partners[0, s] == target).astype(jnp.int32)
            slot += hit * s
            present += hit
            marked += hit * marks[0, s]
        marked_total += marked
        present_total += present
        empty = jnp.where(present > 0, block_rows, 2 * block_rows)
        rows = jnp.where(marked > 0, neighbors[slot], empty).astype(jnp.float32)
        filler = jnp.zeros((pad - knn, block_rows), jnp.float32)
        entry = jnp.concatenate([rows, filler], axis=0).astype(jnp.bfloat16)
        own[place] = entry
        row, column = list_spot(groups, abs(offset), block_rows, pad)
        for message in (right, left) if offset == half else (right,) if offset > 0 else (left,):
            message[row : row + pad, column : column + block_rows] = entry
    lane = lax.broadcasted_iota(jnp.int32, base.shape, 1)
    edges = marked_total.astype(jnp.float32) * float(knn * block_rows)
    entries = present_total.astype(jnp.float32) * float(block_rows * block_rows)
    base[...] = jnp.where(lane == 2, edges, jnp.where(lane == 3, entries, 0.0))
    copies[3].wait()
    wide = local[...].astype(jnp.float32)
    high, low = split(wide * wide)
    ones = jnp.ones((8, wide.shape[1]), jnp.bfloat16)
    norms = lax.dot_general(ones, high, NT, preferred_element_type=jnp.float32)
    norms += lax.dot_general(ones, low, NT, preferred_element_type=jnp.float32)
    for message in (right, left):
        for k, part in enumerate(split(norms[0:1, :])):
            message[knn : knn + 1, k * block_rows : (k + 1) * block_rows] = part


def join_body(pad, right_block, left_block, right_lists, left_lists, right, left):
    block_rows = right_block.shape[0]
    for block, lists, out in ((right_block, right_lists, right), (left_block, left_lists, left)):
        out[0:pad, :] = lists[0:pad, :]
        out[pad : pad + block_rows, :] = block[...]
        kept = out.shape[0] - block_rows
        if kept > pad:
            out[pad + block_rows :, :] = lists[pad:kept, :]


def histogram(entry, knn, block_rows):
    width = 4 if knn < 16 else 8
    per = 32 // width
    shift = {4: 3, 8: 2}[width]
    value = entry.astype(jnp.float32).astype(jnp.int32)
    word = value >> shift
    bit = jnp.left_shift(jnp.int32(1), (value & (per - 1)) * width)
    words = block_rows // per
    index = lax.broadcasted_iota(jnp.int32, (words, block_rows), 0)
    total = jnp.zeros((words, block_rows), jnp.int32)
    for k in range(knn):
        total += jnp.where(word[k : k + 1, :] == index, bit[k : k + 1, :], 0)
    amount = (lax.broadcasted_iota(jnp.int32, (words, per, block_rows), 1)) * width
    spread = jnp.broadcast_to(total[:, None, :], (words, per, block_rows))
    counts = lax.shift_right_logical(spread, amount) & ((1 << width) - 1)
    return counts.reshape(block_rows, block_rows)


def own_counts_body(knn, own, out):
    block_rows = out.shape[1]
    for place in range(out.shape[0]):
        counts = histogram(own[place], knn, block_rows)
        out[place] = counts.astype(jnp.float32).astype(out.dtype)


def split(weight):
    high = weight.astype(jnp.bfloat16)
    return high, (weight - high.astype(jnp.float32)).astype(jnp.bfloat16)


NT = (((1,), (1,)), ((), ()))


def rows_of(refs, pieces):
    parts = [refs[k][a:b, :] for k, a, b in pieces]
    return parts[0] if len(parts) == 1 else jnp.concatenate(parts, axis=0)


def entry_of(refs, spot, pad, block_rows):
    k, row, column = spot
    return refs[k][row : row + pad, column : column + block_rows]


def identity_of(rows):
    row = lax.broadcasted_iota(jnp.int32, (rows, rows), 0)
    column = lax.broadcasted_iota(jnp.int32, (rows, rows), 1)
    return jnp.where(row == column, 1.0, 0.0).astype(jnp.bfloat16)


def transposed(counts):
    return lax.dot_general(identity_of(counts.shape[0]), counts, NT, preferred_element_type=jnp.float32)


def norm_parts(message, knn, block_rows):
    row = message[knn : knn + 1, :].astype(jnp.float32)
    return row[:, :block_rows], row[:, block_rows:]


def norm_table(parts, features, mine):
    high = float(features >> max(features.bit_length() - 8, 0) << max(features.bit_length() - 8, 0))
    fixed = (1.0, 1.0, high, features - high) if mine else (1.0, 1.0, 1.0, 1.0)
    own_first = 0 if mine else 2
    block_rows = parts[0].shape[1]
    row = lax.broadcasted_iota(jnp.int32, (16, block_rows), 0)
    table = jnp.zeros((16, block_rows), jnp.float32)
    for k, value in ((2 - own_first, fixed[0]), (3 - own_first, fixed[1]), (4, fixed[2]), (5, fixed[3])):
        table = jnp.where(row == k, value, table)
    for k, part in enumerate(parts):
        table = jnp.where(row == own_first + k, part, table)
    return table.astype(jnp.bfloat16)


TN = (((0,), (0,)), ((), ()))
CHUNK = 32


def fold(value):
    rows, lanes = value.shape
    return jnp.sum(value.reshape(rows // 8, 8, lanes), axis=0)


def kernel_phase(a, a_norms, b, b_norms, present, counts, constants, out, totals, weight=1.0):
    features = constants[0]
    base = lax.dot_general(
        norm_table(a_norms, features, True),
        norm_table(b_norms, features, False),
        TN,
        preferred_element_type=jnp.float32,
    )
    inner = lax.dot_general(a * -2.0, b, NT, preferred_element_type=jnp.float32)
    block_rows = a.shape[0]
    for start in range(0, block_rows, CHUNK):
        rows = slice(start, start + CHUNK)
        scaled = base[rows] + inner[rows]
        kernel = (present * (features * weight)) / scaled
        if out is not None:
            out[rows, :] = kernel
        if totals is not None:
            logs = jnp.log(scaled * (1.0 / features))
            totals[0] += fold(kernel)
            totals[1] += fold((weight * counts[rows]) * logs)


def pull_phase(remote, kernel, counts, weights, pulls_in, rows_in, pulls, row_sums):
    block_rows = remote.shape[0]
    for start in range(0, block_rows, CHUNK):
        rows = slice(start, start + CHUNK)
        value = kernel[rows, :]
        near = counts[rows, :].astype(jnp.float32) * value
        far = value * value
        for k, weight in enumerate((near, far)):
            total = jnp.sum(weight, axis=1, keepdims=True)
            if rows_in is not None:
                total += rows_in[k, rows, :]
            row_sums[k, rows, :] = total
        high, low = split(near)
        for k, part in enumerate((high, low, far.astype(jnp.bfloat16))):
            weights[k * block_rows + start : k * block_rows + start + CHUNK, :] = part
    product = jnp.dot(weights[...], remote, preferred_element_type=jnp.float32)
    near = product[:block_rows] + product[block_rows : 2 * block_rows]
    far = product[2 * block_rows :]
    pulls[0] = near if pulls_in is None else near + pulls_in[0]
    pulls[1] = far if pulls_in is None else far + pulls_in[1]


def tile_counts(own, entry, knn):
    back = histogram(entry, knn, own.shape[0]).astype(jnp.float32)
    present = jnp.where(entry[0:1, :].astype(jnp.float32) <= float(own.shape[0]), 1.0, 0.0)
    return transposed(own) + back, present


def step_body(tiles, counted, first, constants, *refs):
    _, knn, pad = constants
    local_ref, note_ref, own_ref = refs[:3]
    kernel, weights = refs[-2:]
    held_count = 3 if counted else 2
    held = refs[-2 - held_count : -2]
    held_in = [None] * 3 if first else refs[-2 - 2 * held_count : -2 - held_count]
    sources = refs[3 : len(refs) - 2 - held_count * (1 if first else 2)]
    local = local_ref[...]
    block_rows = local.shape[0]
    local_norms = norm_parts(note_ref, knn, block_rows)
    totals = None
    if counted:
        if first:
            zero = jnp.zeros((8, block_rows), jnp.float32)
            totals = [zero, zero]
        else:
            totals = [held_in[2][0], held_in[2][1]]
    for number, (place, pieces, front, spot) in enumerate(tiles):
        remote = rows_of(sources, pieces)
        entry = entry_of(sources, spot, pad, block_rows)
        counts, present = tile_counts(own_ref[place], entry, knn)
        remote_norms = norm_parts(sources[front], knn, block_rows)
        kernel_phase(local, local_norms, remote, remote_norms, present, counts, constants, kernel, totals)
        before = held if number else held_in
        pull_phase(remote, kernel, counts, weights, before[0], before[1], held[0], held[1])
    if counted:
        held[2][0] = totals[0]
        held[2][1] = totals[1]


def sums_body(tiles, pairs, constants, *refs):
    _, knn, pad = constants
    local_ref, note_ref, own_ref, base_ref, sums_in = refs[:5]
    row_ref, kernels, all_counts = refs[-3:]
    sources = refs[5:-3]
    local = local_ref[...]
    block_rows = local.shape[0]
    local_norms = norm_parts(note_ref, knn, block_rows)
    totals = [sums_in[0], sums_in[1]]
    for number, (place, pieces, front, spot) in enumerate(tiles):
        remote = rows_of(sources, pieces)
        entry = entry_of(sources, spot, pad, block_rows)
        counts, present = tile_counts(own_ref[place], entry, knn)
        all_counts[number] = counts.astype(all_counts.dtype)
        remote_norms = norm_parts(sources[front], knn, block_rows)
        kernel_phase(
            local, local_norms, remote, remote_norms, present, counts, constants, kernels.at[number], totals
        )
    for left_pieces, left_front, right_pieces, right_front, there, back, weight in pairs:
        entry = entry_of(sources, there, pad, block_rows)
        forward = histogram(entry, knn, block_rows).astype(jnp.float32).astype(jnp.bfloat16)
        counts, present = tile_counts(forward, entry_of(sources, back, pad, block_rows), knn)
        kernel_phase(
            rows_of(sources, left_pieces),
            norm_parts(sources[left_front], knn, block_rows),
            rows_of(sources, right_pieces),
            norm_parts(sources[right_front], knn, block_rows),
            present,
            counts,
            constants,
            None,
            totals,
            weight,
        )
    lane = lax.broadcasted_iota(jnp.int32, row_ref.shape, 1)
    row = jnp.where(lane == 0, jnp.sum(totals[0]), base_ref[...])
    row_ref[...] = jnp.where(lane == 1, jnp.sum(totals[1]) * -0.5, row)


def pull_body(tiles, *refs):
    kernels, counts = refs[:2]
    pulls_in, rows_in, pulls, row_sums, weights = refs[-5:]
    sources = refs[2:-5]
    for number, (_, pieces, _, _) in enumerate(tiles):
        before = (pulls, row_sums) if number else (pulls_in, rows_in)
        pull_phase(
            rows_of(sources, pieces), kernels.at[number], counts.at[number], weights, *before, pulls, row_sums
        )


def finish_body(groups, features, table, *refs):
    windows = refs[: len(table)]
    local_ref, pulls, row_sums, gradient, loss, relative = refs[len(table) :]
    for ref, rows in zip(windows, table):
        for row, offset in rows:
            relative[offset : offset + 1, :] = ref[row : row + 1, :]
    me = ring_position(lax.axis_index("wide"), groups)
    summed = jnp.sum(pltpu.roll(relative[...], me, 0), axis=0, keepdims=True)
    lane = lax.broadcasted_iota(jnp.int32, summed.shape, 1)

    def pick(k):
        return jnp.sum(jnp.where(lane == k, summed, 0.0), axis=1, keepdims=True)

    total, attract, edges, entries = pick(0), pick(1), pick(2), pick(3)
    loss[...] = -attract / edges + jnp.log(total / entries)
    repulsion = 2.0 * edges / total
    scale = 2.0 / features
    near_scale, far_scale = scale, scale * repulsion
    for start in range(0, gradient.shape[0], CHUNK):
        chunk = slice(start, start + CHUNK)
        rows = near_scale * row_sums[0, chunk, :] - far_scale * row_sums[1, chunk, :]
        pull = near_scale * pulls[0, chunk, :] - far_scale * pulls[1, chunk, :]
        gradient[chunk, :] = rows * local_ref[chunk, :].astype(jnp.float32) - pull


def column_step(embeddings, partners, pair_kind, neighbors):
    block_rows, features = embeddings.shape
    knn = neighbors.shape[1]
    pad = list_rows(knn)
    groups = lax.axis_size("wide")
    half, quarter = groups // 2, groups // 4
    offsets = ring_offsets(groups)
    places = len(offsets)
    place_of = {offset: place for place, offset in enumerate(offsets)}
    tails = tail_groups(groups)
    list_height = pad * (len(tails) + 1)
    lists = jax.ShapeDtypeStruct((list_height, features), embeddings.dtype)

    def send(value, offset):
        return lax.ppermute(value, "wide", shift_pairs(groups, offset))

    def both(right, left):
        return [send(right, 1), send(left, -1)]

    def height(step):
        return pad * (1 + sum(far >= step for _, far in tails))

    blocks = both(embeddings, embeddings)
    right_note, left_note, own, base, local = pl.pallas_call(
        functools.partial(prepare_body, groups, offsets),
        out_shape=[
            lists,
            lists,
            jax.ShapeDtypeStruct((places, pad, block_rows), jnp.bfloat16),
            jax.ShapeDtypeStruct((1, 128), jnp.float32),
            jax.ShapeDtypeStruct(embeddings.shape, embeddings.dtype),
        ],
        in_specs=[pl.BlockSpec(memory_space=pltpu.HBM)] * 4,
        out_specs=[VMEM] * 5,
        scratch_shapes=[
            pltpu.SMEM(partners.shape, jnp.int32),
            pltpu.SMEM(pair_kind.shape, jnp.int32),
            pltpu.VMEM(neighbors.shape, jnp.int32),
            pltpu.SemaphoreType.DMA((4,)),
        ],
        compiler_params=compiler_params(8),
        cost_estimate=cost(1.5),
        name="prepare",
    )(*(pltpu.with_memory_space_constraint(x, pltpu.HBM) for x in (partners, pair_kind, neighbors, embeddings)))
    notes = both(right_note, left_note)
    own_counts = pl.pallas_call(
        functools.partial(own_counts_body, knn),
        out_shape=jax.ShapeDtypeStruct((places, block_rows, block_rows), jnp.bfloat16),
        in_specs=[VMEM],
        out_specs=VMEM,
        compiler_params=compiler_params(8),
        cost_estimate=cost(1.0),
        name="own_counts",
    )(own)
    arrived = {1: blocks + notes}
    for step in range(2, quarter + 1):
        blocks = both(*blocks)
        notes = [
            send(note[: height(step)], sign * step)
            for note, sign in ((right_note, 1), (left_note, -1))
        ]
        arrived[step] = blocks + notes
    message = jax.ShapeDtypeStruct((block_rows + height(quarter + 1), features), embeddings.dtype)
    right, left = pl.pallas_call(
        functools.partial(join_body, pad),
        out_shape=[message, message],
        in_specs=[VMEM] * 4,
        out_specs=[VMEM] * 2,
        compiler_params=compiler_params(4),
        cost_estimate=cost(0.3),
        name="join",
    )(*blocks, *notes)
    for step in range(quarter + 1, half):
        keep = block_rows + height(step)
        right, left = arrived[step] = both(right[:keep], left[:keep])
    middle = pad + block_rows // 2
    arrived[half] = both(right[:middle], left[middle : pad + block_rows])

    def spot_of(step, side, distance):
        row, column = list_spot(groups, distance, block_rows, pad)
        if step <= quarter:
            return side + 2, row, column
        return side, row + (block_rows if row else 0), column

    def block_of(step, side):
        start = 0 if step <= quarter else pad
        return [(side, start, start + block_rows)]

    def front_of(step, side):
        return side + 2 if step <= quarter else side

    def tiles_of(step):
        if step == half:
            pieces = [(0, pad, middle), (1, 0, block_rows // 2)]
            return [(place_of[half], pieces, 0, spot_of(step, 0, half))]
        return [
            (place_of[sign * step], block_of(step, side), front_of(step, side), spot_of(step, side, step))
            for side, sign in ((0, -1), (1, 1))
        ]

    def call(body, operands, shapes, time, aliases=None, scratch=()):
        return pl.pallas_call(
            body,
            out_shape=shapes,
            in_specs=[VMEM] * len(operands),
            out_specs=[VMEM] * len(shapes),
            scratch_shapes=list(scratch),
            input_output_aliases=aliases or {},
            compiler_params=compiler_params(12),
            cost_estimate=cost(time),
        )(*operands)

    constants = (features, knn, pad)
    square = (block_rows, block_rows)
    scratch = [
        pltpu.VMEM(square, jnp.float32),
        pltpu.VMEM((3 * block_rows, block_rows), jnp.bfloat16),
    ]
    held = [
        jax.ShapeDtypeStruct((2, block_rows, features), jnp.float32),
        jax.ShapeDtypeStruct((2, block_rows, 1), jnp.float32),
        jax.ShapeDtypeStruct((2, 8, block_rows), jnp.float32),
    ]
    common = [local, right_note, own_counts]
    state = None
    for step in range(1, half + 1):
        tiles = tiles_of(step)
        if step == quarter:
            sources, pairs = list(arrived[step]), []
            for distance in range(quarter + 1, half + 1):
                lower = distance - quarter
                at, front, factor = 0, 2, 1.0
                if lower != quarter:
                    at, front, factor = len(sources), len(sources) + 1, 2.0
                    sources += [arrived[lower][0], arrived[lower][2]]
                there = (front,) + spot_of(step, 0, distance)[1:]
                pairs.append(
                    (
                        block_of(step, at),
                        front,
                        block_of(step, 1),
                        3,
                        there,
                        spot_of(step, 1, distance),
                        factor,
                    )
                )
            window, kernels, counts = call(
                functools.partial(sums_body, tiles, pairs, constants),
                common + [base, state[2]] + sources,
                [
                    jax.ShapeDtypeStruct((1, 128), jnp.float32),
                    jax.ShapeDtypeStruct((2, *square), jnp.float32),
                    jax.ShapeDtypeStruct((2, *square), jnp.bfloat16),
                ],
                1.8,
            )
            operands = [kernels, counts] + arrived[step][:2]
            state = call(
                functools.partial(pull_body, tiles),
                operands + list(state[:2]),
                held[:2],
                1.5,
                {len(operands) + k: k for k in range(2)},
                scratch[1:],
            )
            continue
        counted = step < quarter
        operands = common + arrived[step]
        shapes = held if counted else held[:2]
        first = state is None
        aliases = {} if first else {len(operands) + k: k for k in range(len(shapes))}
        state = call(
            functools.partial(step_body, tiles, counted, first, constants),
            operands + ([] if first else list(state)),
            shapes,
            2.0,
            aliases,
            scratch,
        )
    columns = lax.axis_size("narrow")
    bit = 1
    while bit < columns:
        other = lax.ppermute(window, "narrow", [(k, k ^ bit) for k in range(columns)])
        window = window + other
        bit *= 2
    reach, received = 0, []
    table = [[(0, 0)]]
    while 2 * reach + 1 < groups:
        if reach:
            window = jnp.concatenate([received[1], window, received[0]], axis=0)
            table = [[(row, (row - reach) % groups) for row in range(2 * reach + 1)]]
        stride = 2 * reach + 1
        received = [send(window, -stride), send(window, stride)]
        seen = {offset for _, offset in table[0]}
        for sign in (1, -1):
            rows = []
            for row in range(2 * reach + 1):
                offset = (sign * stride + row - reach) % groups
                if offset not in seen:
                    seen.add(offset)
                    rows.append((row, offset))
            table.append(rows)
        reach = 3 * reach + 1
    gradient, loss = call(
        functools.partial(finish_body, groups, features, table),
        [window, *received, local, *state],
        [
            jax.ShapeDtypeStruct((block_rows, features), jnp.float32),
            jax.ShapeDtypeStruct((1, 1), jnp.float32),
        ],
        1.0,
        None,
        [pltpu.VMEM((groups, 128), jnp.float32)],
    )
    return gradient, loss.reshape(())


def solution(mesh):
    in_specs = (P(AXES, None), P(AXES, None), P(AXES, None), P(None, None, AXES))
    return jax.shard_map(
        column_step, mesh=mesh, in_specs=in_specs, out_specs=(P(AXES, None), P()), check_vma=False
    )
```

time: 52.5 us -> 50.5 us (0.962)
  Pallas kernels: 12.7 us -> 8.86 us
  starting transfers between devices: 20.9 us -> 23.9 us
  waiting for transfers between devices: 17.9 us -> 16.8 us
    pallas_call x5 -> x6, Pallas kernels: 10.2 us -> 6.61 us  [call(): pl.pallas_call(body, out_shape=shapes, in_specs=[VMEM] * len(operands), o...]
    ppermute x16, starting transfers between devices: 19.3 us -> 22.3 us  [send(): return lax.ppermute(value, 'wide', shift_pairs(groups, offset))]
    ppermute x16, waiting for transfers between devices: 14.7 us -> 13.6 us  [send(): return lax.ppermute(value, 'wide', shift_pairs(groups, offset))]
  transfers between devices with their start and end apart: 18 -> 18, of which waited for: 8 -> 8; matrix products, arithmetic and copies ran while one was open for 0% -> 0% of each run, Pallas kernels for 22% -> 15%
where the time goes in v1:
time: 50.5 us; the launch traced here: 50.4 us
  starting transfers between devices  23.9 us (47%)
  waiting for transfers between devices  16.8 us (33%)
  Pallas kernels  8.86 us (18%)
  between operations  0.75 us (1%)
    ppermute x16, starting transfers between devices, send(): return lax.ppermute(value, 'wide', shift_pairs(groups, offset))  22.3 us
    ppermute x16, waiting for transfers between devices, send(): return lax.ppermute(value, 'wide', shift_pairs(groups, offset))  13.6 us
    pallas_call x6, Pallas kernels, call(): pl.pallas_call(body, out_shape=shapes, in_specs=[VMEM] * len(operands), o...  6.61 us
    ppermute x2, waiting for transfers between devices, column_step(): lax.ppermute(window, 'narrow', [(k, k ^ bit) for k in range(columns)])  3.2 us
    ppermute x2, starting transfers between devices, column_step(): lax.ppermute(window, 'narrow', [(k, k ^ bit) for k in range(columns)])  1.58 us
    pallas_call x1, Pallas kernels, column_step(): pl.pallas_call(functools.partial(prepare_body, groups, offsets), out_shap...  1.32 us
  transfers between devices with their start and end apart: 18, of which 8 were waited for; matrix products, arithmetic and copies ran while one was open for 0% of the time, Pallas kernels for 15%

profile of v1, /device:TPU:0, one launch (start us, length us, event | category | flops | bytes accessed | tf_op | source)
XLA Modules:
  0.0 50.4 jit_solution(6214514547472777805)
XLA Ops:
  0.6 3.1 %collective-permute-start = (bf16[256,512]{1,0:T(8,128)(2,1)}, bf16[256,512]{1,0:T(8,128)(2,1)S(1)}, u32[]{:S(2)}, u32[]{:S(2)}) collective-permute-start(bf16[256,512]{1,0:T(8,128)(2,1)} %refs_3_.1), channel_id=1, source_target_pairs={{0,8},{8,16},{16,24},{24,28},{28,20},{20,12},{12,4},{4,0},{1,9},{9... | collective-permute-start | bytes 786440 | tf_op jit(solution)/shard_map/ppermute | solution.py:385
  3.7 0.0 collective-permute-start.1
  3.7 6.4 %collective-permute-done.refs_3_.refs_9_ = bf16[256,512]{1,0:T(8,128)(2,1)S(1)} collective-permute-done((bf16[256,512]{1,0:T(8,128)(2,1)}, bf16[256,512]{1,0:T(8,128)(2,1)S(1)}, u32[]{:S(2)}, u32[]{:S(2)}) %collective-permute-start) | collective-permute-done | bytes 262176 | tf_op jit(solution)/shard_map/ppermute | solution.py:385
  10.2 1.8 %collective-permute-start.4 = (bf16[256,512]{1,0:T(8,128)(2,1)S(1)}, bf16[256,512]{1,0:T(8,128)(2,1)S(1)}, u32[]{:S(2)}, u32[]{:S(2)}) collective-permute-start(bf16[256,512]{1,0:T(8,128)(2,1)S(1)} %collective-permute-done.refs_3_.refs_9_), channel_id=1, source_target_pairs={{0,8},{8,16},{16,24},{24,28},{28,20},{20,12},{12,4},{4,0},{1,9},{9... | collective-permute-start | bytes 786440 | tf_op jit(solution)/shard_map/ppermute | solution.py:385
  12.0 0.0 collective-permute-done.1.refs_4_
  12.0 0.2 collective-permute-start.5
  12.2 1.3 %prepare.1 = (bf16[32,512]{1,0:T(8,128)(2,1)S(1)}, bf16[32,512]{1,0:T(8,128)(2,1)S(1)}, bf16[7,16,256]{2,1,0:T(8,128)(2,1)S(1)}, f32[1,128]{1,0:T(1,128)S(1)}, bf16[256,512]{1,0:T(8,128)(2,1)S(1)}) custom-call(s32[1,7]{1,0:T(1,128)} %refs_0_.1, s32[1,7]{1,0:T(1,128)} %refs_1_.1, s32[7,15,256]{2,1,0:T(8,128)} %refs_2_.1, bf16[256,512]{1,0:T(8,128)(2,1)} %refs_3_.1), custom_call_target="tpu_custom_call" | custom-call | flops 1200000000 | bytes 3000000 | tf_op jit(solution)/shard_map/prepare/pallas_call | solution.py:394
  13.5 1.9 %collective-permute-start.2 = (bf16[32,512]{1,0:T(8,128)(2,1)S(1)}, bf16[32,512]{1,0:T(8,128)(2,1)S(1)}, u32[]{:S(2)}, u32[]{:S(2)}) collective-permute-start(bf16[32,512]{1,0:T(8,128)(2,1)S(1)} %get-tuple-element.24.refs_1_), channel_id=1, source_target_pairs={{0,8},{8,16},{16,24},{24,28},{28,20},{20,12},{12,4},{4,0},{1,9},{9... | collective-permute-start | bytes 98312 | tf_op jit(solution)/shard_map/ppermute | solution.py:385
  15.4 2.6 %collective-permute-start.6 = (bf16[32,512]{1,0:T(8,128)(2,1)S(1)}, bf16[32,512]{1,0:T(8,128)(2,1)S(1)}, u32[]{:S(2)}, u32[]{:S(2)}) collective-permute-start(bf16[32,512]{1,0:T(8,128)(2,1)S(1)} %get-tuple-element.24.refs_1_), channel_id=1, source_target_pairs={{0,16},{8,24},{16,28},{24,20},{28,12},{20,4},{12,0},{4,8},{1,17},{... | collective-permute-start | bytes 98312 | tf_op jit(solution)/shard_map/ppermute | solution.py:385
  18.0 0.5 collective-permute-start.3
  18.4 0.9 %own_counts.1.refs_2_ = bf16[7,256,256]{2,1,0:T(8,128)(2,1)S(1)} custom-call(bf16[7,16,256]{2,1,0:T(8,128)(2,1)S(1)} %get-tuple-element.25.own), custom_call_target="tpu_custom_call" | custom-call | flops 800000000 | bytes 2000000 | tf_op jit(solution)/shard_map/own_counts/pallas_call | solution.py:416
  19.3 0.0 collective-permute-done.2.refs_5_.refs_10_
  19.3 2.2 %collective-permute-start.7 = (bf16[32,512]{1,0:T(8,128)(2,1)S(1)}, bf16[32,512]{1,0:T(8,128)(2,1)S(1)}, u32[]{:S(2)}, u32[]{:S(2)}) collective-permute-start(bf16[32,512]{1,0:T(8,128)(2,1)S(1)} %get-tuple-element.27), channel_id=1, source_target_pairs={{0,12},{8,4},{16,0},{24,8},{28,16},{20,24},{12,28},{4,20},{1,13},{... | collective-permute-start | bytes 98312 | tf_op jit(solution)/shard_map/ppermute | solution.py:385
  21.5 0.4 collective-permute-done.3.refs_6_
  21.9 1.3 %shard_map.59 = (f32[2,256,512]{2,1,0:T(8,128)S(1)}, f32[2,256,1]{2,1,0:T(8,128)S(1)}, f32[2,8,256]{2,1,0:T(8,128)S(1)}) custom-call(bf16[256,512]{1,0:T(8,128)(2,1)S(1)} %get-tuple-element.23.refs_0_.refs_3_, bf16[32,512]{1,0:T(8,128)(2,1)S(1)} %get-tuple-element.24.refs_1_, bf16[7,256,256]{2,1,0:T(8,128)(2,1)S(1)} %own_counts.1.refs_2_, ...), custom_call_target="tpu_custom_call" | custom-call | flops 1600000000 | bytes 4000000 | tf_op jit(solution)/shard_map/pallas_call | solution.py:472
  23.2 0.0 collective-permute-done.6.refs_7_.right_lists
  23.2 1.0 %collective-permute-done.7.refs_8_.left_lists = bf16[32,512]{1,0:T(8,128)(2,1)S(1)} collective-permute-done((bf16[32,512]{1,0:T(8,128)(2,1)S(1)}, bf16[32,512]{1,0:T(8,128)(2,1)S(1)}, u32[]{:S(2)}, u32[]{:S(2)}) %collective-permute-start.7) | collective-permute-done | bytes 32800 | tf_op jit(solution)/shard_map/ppermute | solution.py:385
  24.2 0.0 collective-permute-done.4.refs_5_.right_block.refs_2_
  24.2 0.0 collective-permute-done.5.refs_6_.left_block.refs_3_
  24.3 1.6 %collective-permute-start.14 = (bf16[272,512]{1,0:T(8,128)(2,1)S(1)}, bf16[272,512]{1,0:T(8,128)(2,1)S(1)}, u32[]{:S(2)}, u32[]{:S(2)}) collective-permute-start(bf16[272,512]{1,0:T(8,128)(2,1)S(1)} %get-tuple-element.30), channel_id=1, source_target_pairs={{0,8},{8,16},{16,24},{24,28},{28,20},{20,12},{12,4},{4,0},{1,9},{9... | collective-permute-start | bytes 835592 | tf_op jit(solution)/shard_map/ppermute | solution.py:385
  25.9 0.5 collective-permute-start.16
  26.3 1.6 %shard_map.60 = (f32[1,128]{1,0:T(1,128)S(1)}, f32[2,256,256]{2,1,0:T(8,128)S(1)}, bf16[2,256,256]{2,1,0:T(8,128)(2,1)S(1)}) custom-call(bf16[256,512]{1,0:T(8,128)(2,1)S(1)} %get-tuple-element.23.refs_0_.refs_3_, bf16[32,512]{1,0:T(8,128)(2,1)S(1)} %get-tuple-element.24.refs_1_, bf16[7,256,256]{2,1,0:T(8,128)(2,1)S(1)} %own_counts.1.refs_2_, ...), custom_call_target="tpu_custom_call" | custom-call | flops 1440000000 | bytes 3600000 | tf_op jit(solution)/shard_map/pallas_call | solution.py:472
  27.9 0.1 collective-permute-start.8
  28.0 1.1 %collective-permute-done.8 = f32[1,128]{1,0:T(1,128)S(1)} collective-permute-done((f32[1,128]{1,0:T(1,128)S(1)}, f32[1,128]{1,0:T(1,128)S(1)}, u32[]{:S(2)}, u32[]{:S(2)}) %collective-permute-start.8) | collective-permute-done | bytes 544 | tf_op jit(solution)/shard_map/ppermute | solution.py:554
  29.2 1.5 %collective-permute-start.9 = (f32[1,128]{1,0:T(1,128)S(1)}, f32[1,128]{1,0:T(1,128)S(1)}, u32[]{:S(2)}, u32[]{:S(2)}) collective-permute-start(f32[1,128]{1,0:T(1,128)S(1)} %add.6), channel_id=1, source_target_pairs={{0,2},{1,3},{2,0},{3,1},{4,6},{5,7},{6,4},{7,5},{8,10},{9,11},{10,... | collective-permute-start | bytes 1544 | tf_op jit(solution)/shard_map/ppermute | solution.py:554
  30.7 2.1 %collective-permute-done.9 = f32[1,128]{1,0:T(1,128)S(1)} collective-permute-done((f32[1,128]{1,0:T(1,128)S(1)}, f32[1,128]{1,0:T(1,128)S(1)}, u32[]{:S(2)}, u32[]{:S(2)}) %collective-permute-start.9) | collective-permute-done | bytes 544 | tf_op jit(solution)/shard_map/ppermute | solution.py:554
  32.7 1.6 %collective-permute-start.10 = (f32[1,128]{1,0:T(1,128)S(1)}, f32[1,128]{1,0:T(1,128)S(1)}, u32[]{:S(2)}, u32[]{:S(2)}) collective-permute-start(f32[1,128]{1,0:T(1,128)S(1)} %add.7), channel_id=1, source_target_pairs={{0,8},{8,16},{16,24},{24,28},{28,20},{20,12},{12,4},{4,0},{1,9},{9... | collective-permute-start | bytes 1544 | tf_op jit(solution)/shard_map/ppermute | solution.py:385
  34.3 0.5 collective-permute-start.11
  34.8 0.7 %shard_map.61 = (f32[2,256,512]{2,1,0:T(8,128)S(1)}, f32[2,256,1]{2,1,0:T(8,128)S(1)}) custom-call(f32[2,256,256]{2,1,0:T(8,128)S(1)} %get-tuple-element.32.refs_0_, bf16[2,256,256]{2,1,0:T(8,128)(2,1)S(1)} %get-tuple-element.33.refs_1_, ...), custom_call_target="tpu_custom_call", output_to_operand_aliasing={{0}: (4, {}), {1}: (5, {})} | custom-call | flops 1200000000 | bytes 3000000 | tf_op jit(solution)/shard_map/pallas_call | solution.py:472
  35.4 0.9 %collective-permute-done.10 = f32[1,128]{1,0:T(1,128)S(1)} collective-permute-done((f32[1,128]{1,0:T(1,128)S(1)}, f32[1,128]{1,0:T(1,128)S(1)}, u32[]{:S(2)}, u32[]{:S(2)}) %collective-permute-start.10) | collective-permute-done | bytes 544 | tf_op jit(solution)/shard_map/ppermute | solution.py:385
  36.3 1.6 %collective-permute-done.11 = f32[1,128]{1,0:T(1,128)S(1)} collective-permute-done((f32[1,128]{1,0:T(1,128)S(1)}, f32[1,128]{1,0:T(1,128)S(1)}, u32[]{:S(2)}, u32[]{:S(2)}) %collective-permute-start.11) | collective-permute-done | bytes 544 | tf_op jit(solution)/shard_map/ppermute | solution.py:385
  37.9 2.2 %collective-permute-start.12 = (f32[3,128]{1,0:T(4,128)S(1)}, f32[3,128]{1,0:T(4,128)S(1)}, u32[]{:S(2)}, u32[]{:S(2)}) collective-permute-start(f32[3,128]{1,0:T(4,128)S(1)} %pad_maximum_fusion.refs_0_), channel_id=1, source_target_pairs={{0,20},{8,12},{16,4},{24,0},{28,8},{20,16},{12,24},{4,28},{1,21},{... | collective-permute-start | bytes 4616 | tf_op jit(solution)/shard_map/ppermute | solution.py:385
  40.1 1.7 %collective-permute-start.13 = (f32[3,128]{1,0:T(4,128)S(1)}, f32[3,128]{1,0:T(4,128)S(1)}, u32[]{:S(2)}, u32[]{:S(2)}) collective-permute-start(f32[3,128]{1,0:T(4,128)S(1)} %pad_maximum_fusion.refs_0_), channel_id=1, source_target_pairs={{0,24},{8,28},{16,20},{24,12},{28,4},{20,0},{12,8},{4,16},{1,25},{... | collective-permute-start | bytes 4616 | tf_op jit(solution)/shard_map/ppermute | solution.py:385
  41.8 0.0 collective-permute-done.14.refs_3_
  41.8 1.6 %collective-permute-start.15 = (bf16[144,512]{1,0:T(8,128)(2,1)S(1)}, bf16[144,512]{1,0:T(8,128)(2,1)S(1)}, u32[]{:S(2)}, u32[]{:S(2)}) collective-permute-start(bf16[144,512]{1,0:T(8,128)(2,1)S(1)} %slice.8), channel_id=1, source_target_pairs={{0,8},{8,16},{16,24},{24,28},{28,20},{20,12},{12,4},{4,0},{1,9},{9... | collective-permute-start | bytes 442376 | tf_op jit(solution)/shard_map/ppermute | solution.py:385
  43.4 0.0 collective-permute-done.16.refs_4_
  43.4 0.5 collective-permute-start.17
  43.9 1.3 %shard_map.62 = (f32[2,256,512]{2,1,0:T(8,128)S(1)}, f32[2,256,1]{2,1,0:T(8,128)S(1)}) custom-call(bf16[256,512]{1,0:T(8,128)(2,1)S(1)} %get-tuple-element.23.refs_0_.refs_3_, bf16[32,512]{1,0:T(8,128)(2,1)S(1)} %get-tuple-element.24.refs_1_, bf16[7,256,256]{2,1,0:T(8,128)(2,1)S(1)} %own_counts.1.refs_2_, ...), custom_call_target="tpu_custom_call", output_to_operand_aliasing={{0}: (5, {}), {1}: (6, {})} | custom-call | flops 1600000000 | bytes 4000000 | tf_op jit(solution)/shard_map/pallas_call | solution.py:472
  45.2 3.3 %collective-permute-done.17.refs_4_ = bf16[128,512]{1,0:T(8,128)(2,1)S(1)} collective-permute-done((bf16[128,512]{1,0:T(8,128)(2,1)S(1)}, bf16[128,512]{1,0:T(8,128)(2,1)S(1)}, u32[]{:S(2)}, u32[]{:S(2)}) %collective-permute-start.17) | collective-permute-done | bytes 131104 | tf_op jit(solution)/shard_map/ppermute | solution.py:385
  48.5 0.0 collective-permute-done.15.refs_3_
  48.5 0.8 %shard_map.63 = (f32[2,256,512]{2,1,0:T(8,128)S(1)}, f32[2,256,1]{2,1,0:T(8,128)S(1)}) custom-call(bf16[256,512]{1,0:T(8,128)(2,1)S(1)} %get-tuple-element.23.refs_0_.refs_3_, bf16[32,512]{1,0:T(8,128)(2,1)S(1)} %get-tuple-element.24.refs_1_, bf16[7,256,256]{2,1,0:T(8,128)(2,1)S(1)} %own_counts.1.refs_2_, ...), custom_call_target="tpu_custom_call", output_to_operand_aliasing={{0}: (5, {}), {1}: (6, {})} | custom-call | flops 1600000000 | bytes 4000000 | tf_op jit(solution)/shard_map/pallas_call | solution.py:472
  49.3 0.0 collective-permute-done.12.refs_1_
  49.3 0.0 collective-permute-done.13.refs_2_
  49.3 1.1 %shard_map.64 = (f32[256,512]{1,0:T(8,128)}, f32[1,1]{1,0:T(1,128)}) custom-call(f32[3,128]{1,0:T(4,128)S(1)} %pad_maximum_fusion.refs_0_, f32[3,128]{1,0:T(4,128)S(1)} %collective-permute-done.12.refs_1_, f32[3,128]{1,0:T(4,128)S(1)} %collective-permute-done.13.refs_2_, bf16[256,512]{1,0:T(8,128)(2,1)S(1)} %get-tuple-element.23.refs_0_.refs_3_, ...), custom_call_target="tpu_custom_call" | custom-call | flops 800000000 | bytes 2000000 | tf_op jit(solution)/shard_map/pallas_call | solution.py:472
  (6 shorter events, 0.1 us)
Async XLA Ops:
  0.6 9.5 %collective-permute-start = (bf16[256,512]{1,0:T(8,128)(2,1)}, bf16[256,512]{1,0:T(8,128)(2,1)S(1)}, u32[]{:S(2)}, u32[]{:S(2)}) collective-permute-start(bf16[256,512]{1,0:T(8,128)(2,1)} %refs_3_.1), channel_id=1, source_target_pairs={{0,8},{8,16},{16,24},{24,28},{28,20},{20,12},{12,4},{4,0},{1,9},{9... | collective-permute-start | bytes 786440 | tf_op jit(solution)/shard_map/ppermute | solution.py:385
  3.7 8.3 %collective-permute-start.1 = (bf16[256,512]{1,0:T(8,128)(2,1)}, bf16[256,512]{1,0:T(8,128)(2,1)S(1)}, u32[]{:S(2)}, u32[]{:S(2)}) collective-permute-start(bf16[256,512]{1,0:T(8,128)(2,1)} %refs_3_.1), channel_id=1, source_target_pairs={{0,4},{8,0},{16,8},{24,16},{28,24},{20,28},{12,20},{4,12},{1,5},{9... | collective-permute-start | bytes 786440 | tf_op jit(solution)/shard_map/ppermute | solution.py:385
  10.2 14.0 %collective-permute-start.4 = (bf16[256,512]{1,0:T(8,128)(2,1)S(1)}, bf16[256,512]{1,0:T(8,128)(2,1)S(1)}, u32[]{:S(2)}, u32[]{:S(2)}) collective-permute-start(bf16[256,512]{1,0:T(8,128)(2,1)S(1)} %collective-permute-done.refs_3_.refs_9_), channel_id=1, source_target_pairs={{0,8},{8,16},{16,24},{24,28},{28,20},{20,12},{12,4},{4,0},{1,9},{9... | collective-permute-start | bytes 786440 | tf_op jit(solution)/shard_map/ppermute | solution.py:385
  12.0 12.2 %collective-permute-start.5 = (bf16[256,512]{1,0:T(8,128)(2,1)S(1)}, bf16[256,512]{1,0:T(8,128)(2,1)S(1)}, u32[]{:S(2)}, u32[]{:S(2)}) collective-permute-start(bf16[256,512]{1,0:T(8,128)(2,1)S(1)} %collective-permute-done.1.refs_4_), channel_id=1, source_target_pairs={{0,4},{8,0},{16,8},{24,16},{28,24},{20,28},{12,20},{4,12},{1,5},{9... | collective-permute-start | bytes 786440 | tf_op jit(solution)/shard_map/ppermute | solution.py:385
  13.5 5.8 %collective-permute-start.2 = (bf16[32,512]{1,0:T(8,128)(2,1)S(1)}, bf16[32,512]{1,0:T(8,128)(2,1)S(1)}, u32[]{:S(2)}, u32[]{:S(2)}) collective-permute-start(bf16[32,512]{1,0:T(8,128)(2,1)S(1)} %get-tuple-element.24.refs_1_), channel_id=1, source_target_pairs={{0,8},{8,16},{16,24},{24,28},{28,20},{20,12},{12,4},{4,0},{1,9},{9... | collective-permute-start | bytes 98312 | tf_op jit(solution)/shard_map/ppermute | solution.py:385
  15.4 7.8 %collective-permute-start.6 = (bf16[32,512]{1,0:T(8,128)(2,1)S(1)}, bf16[32,512]{1,0:T(8,128)(2,1)S(1)}, u32[]{:S(2)}, u32[]{:S(2)}) collective-permute-start(bf16[32,512]{1,0:T(8,128)(2,1)S(1)} %get-tuple-element.24.refs_1_), channel_id=1, source_target_pairs={{0,16},{8,24},{16,28},{24,20},{28,12},{20,4},{12,0},{4,8},{1,17},{... | collective-permute-start | bytes 98312 | tf_op jit(solution)/shard_map/ppermute | solution.py:385
  18.0 3.9 %collective-permute-start.3 = (bf16[32,512]{1,0:T(8,128)(2,1)S(1)}, bf16[32,512]{1,0:T(8,128)(2,1)S(1)}, u32[]{:S(2)}, u32[]{:S(2)}) collective-permute-start(bf16[32,512]{1,0:T(8,128)(2,1)S(1)} %get-tuple-element.27), channel_id=1, source_target_pairs={{0,4},{8,0},{16,8},{24,16},{28,24},{20,28},{12,20},{4,12},{1,5},{9... | collective-permute-start | bytes 98312 | tf_op jit(solution)/shard_map/ppermute | solution.py:385
  19.3 4.9 %collective-permute-start.7 = (bf16[32,512]{1,0:T(8,128)(2,1)S(1)}, bf16[32,512]{1,0:T(8,128)(2,1)S(1)}, u32[]{:S(2)}, u32[]{:S(2)}) collective-permute-start(bf16[32,512]{1,0:T(8,128)(2,1)S(1)} %get-tuple-element.27), channel_id=1, source_target_pairs={{0,12},{8,4},{16,0},{24,8},{28,16},{20,24},{12,28},{4,20},{1,13},{... | collective-permute-start | bytes 98312 | tf_op jit(solution)/shard_map/ppermute | solution.py:385
  24.3 17.5 %collective-permute-start.14 = (bf16[272,512]{1,0:T(8,128)(2,1)S(1)}, bf16[272,512]{1,0:T(8,128)(2,1)S(1)}, u32[]{:S(2)}, u32[]{:S(2)}) collective-permute-start(bf16[272,512]{1,0:T(8,128)(2,1)S(1)} %get-tuple-element.30), channel_id=1, source_target_pairs={{0,8},{8,16},{16,24},{24,28},{28,20},{20,12},{12,4},{4,0},{1,9},{9... | collective-permute-start | bytes 835592 | tf_op jit(solution)/shard_map/ppermute | solution.py:385
  25.9 17.5 %collective-permute-start.16 = (bf16[272,512]{1,0:T(8,128)(2,1)S(1)}, bf16[272,512]{1,0:T(8,128)(2,1)S(1)}, u32[]{:S(2)}, u32[]{:S(2)}) collective-permute-start(bf16[272,512]{1,0:T(8,128)(2,1)S(1)} %get-tuple-element.31), channel_id=1, source_target_pairs={{0,4},{8,0},{16,8},{24,16},{28,24},{20,28},{12,20},{4,12},{1,5},{9... | collective-permute-start | bytes 835592 | tf_op jit(solution)/shard_map/ppermute | solution.py:385
  27.9 1.2 %collective-permute-start.8 = (f32[1,128]{1,0:T(1,128)S(1)}, f32[1,128]{1,0:T(1,128)S(1)}, u32[]{:S(2)}, u32[]{:S(2)}) collective-permute-start(f32[1,128]{1,0:T(1,128)S(1)} %get-tuple-element.29), channel_id=1, source_target_pairs={{0,1},{1,0},{2,3},{3,2},{4,5},{5,4},{6,7},{7,6},{8,9},{9,8},{10,11... | collective-permute-start | bytes 1544 | tf_op jit(solution)/shard_map/ppermute | solution.py:554
  29.2 3.6 %collective-permute-start.9 = (f32[1,128]{1,0:T(1,128)S(1)}, f32[1,128]{1,0:T(1,128)S(1)}, u32[]{:S(2)}, u32[]{:S(2)}) collective-permute-start(f32[1,128]{1,0:T(1,128)S(1)} %add.6), channel_id=1, source_target_pairs={{0,2},{1,3},{2,0},{3,1},{4,6},{5,7},{6,4},{7,5},{8,10},{9,11},{10,... | collective-permute-start | bytes 1544 | tf_op jit(solution)/shard_map/ppermute | solution.py:554
  32.7 3.6 %collective-permute-start.10 = (f32[1,128]{1,0:T(1,128)S(1)}, f32[1,128]{1,0:T(1,128)S(1)}, u32[]{:S(2)}, u32[]{:S(2)}) collective-permute-start(f32[1,128]{1,0:T(1,128)S(1)} %add.7), channel_id=1, source_target_pairs={{0,8},{8,16},{16,24},{24,28},{28,20},{20,12},{12,4},{4,0},{1,9},{9... | collective-permute-start | bytes 1544 | tf_op jit(solution)/shard_map/ppermute | solution.py:385
  34.3 3.6 %collective-permute-start.11 = (f32[1,128]{1,0:T(1,128)S(1)}, f32[1,128]{1,0:T(1,128)S(1)}, u32[]{:S(2)}, u32[]{:S(2)}) collective-permute-start(f32[1,128]{1,0:T(1,128)S(1)} %add.7), channel_id=1, source_target_pairs={{0,4},{8,0},{16,8},{24,16},{28,24},{20,28},{12,20},{4,12},{1,5},{9... | collective-permute-start | bytes 1544 | tf_op jit(solution)/shard_map/ppermute | solution.py:385
  37.9 11.4 %collective-permute-start.12 = (f32[3,128]{1,0:T(4,128)S(1)}, f32[3,128]{1,0:T(4,128)S(1)}, u32[]{:S(2)}, u32[]{:S(2)}) collective-permute-start(f32[3,128]{1,0:T(4,128)S(1)} %pad_maximum_fusion.refs_0_), channel_id=1, source_target_pairs={{0,20},{8,12},{16,4},{24,0},{28,8},{20,16},{12,24},{4,28},{1,21},{... | collective-permute-start | bytes 4616 | tf_op jit(solution)/shard_map/ppermute | solution.py:385
  40.1 9.2 %collective-permute-start.13 = (f32[3,128]{1,0:T(4,128)S(1)}, f32[3,128]{1,0:T(4,128)S(1)}, u32[]{:S(2)}, u32[]{:S(2)}) collective-permute-start(f32[3,128]{1,0:T(4,128)S(1)} %pad_maximum_fusion.refs_0_), channel_id=1, source_target_pairs={{0,24},{8,28},{16,20},{24,12},{28,4},{20,0},{12,8},{4,16},{1,25},{... | collective-permute-start | bytes 4616 | tf_op jit(solution)/shard_map/ppermute | solution.py:385
  41.8 6.7 %collective-permute-start.15 = (bf16[144,512]{1,0:T(8,128)(2,1)S(1)}, bf16[144,512]{1,0:T(8,128)(2,1)S(1)}, u32[]{:S(2)}, u32[]{:S(2)}) collective-permute-start(bf16[144,512]{1,0:T(8,128)(2,1)S(1)} %slice.8), channel_id=1, source_target_pairs={{0,8},{8,16},{16,24},{24,28},{28,20},{20,12},{12,4},{4,0},{1,9},{9... | collective-permute-start | bytes 442376 | tf_op jit(solution)/shard_map/ppermute | solution.py:385
  43.4 5.0 %collective-permute-start.17 = (bf16[128,512]{1,0:T(8,128)(2,1)S(1)}, bf16[128,512]{1,0:T(8,128)(2,1)S(1)}, u32[]{:S(2)}, u32[]{:S(2)}) collective-permute-start(bf16[128,512]{1,0:T(8,128)(2,1)S(1)} %slice.9), channel_id=1, source_target_pairs={{0,4},{8,0},{16,8},{24,16},{28,24},{20,28},{12,20},{4,12},{1,5},{9... | collective-permute-start | bytes 393224 | tf_op jit(solution)/shard_map/ppermute | solution.py:385

commit v2 on v1

--- a/solution.py
+++ b/solution.py
@@ -122,13 +122,13 @@
 
 
 def join_body(pad, right_block, left_block, right_lists, left_lists, right, left):
-    block_rows = right_block.shape[0]
+    rows = right_block.shape[0]
     for block, lists, out in ((right_block, right_lists, right), (left_block, left_lists, left)):
         out[0:pad, :] = lists[0:pad, :]
-        out[pad : pad + block_rows, :] = block[...]
-        kept = out.shape[0] - block_rows
+        out[pad : pad + rows, :] = block[...]
+        kept = out.shape[0] - rows
         if kept > pad:
-            out[pad + block_rows :, :] = lists[pad:kept, :]
+            out[pad + rows :, :] = lists[pad:kept, :]
 
 
 def histogram(entry, knn, block_rows):
@@ -422,16 +422,20 @@
         cost_estimate=cost(1.0),
         name="own_counts",
     )(own)
-    arrived = {1: blocks + notes}
+    middle = block_rows // 2
+    halves = [[block[:middle] for block in blocks], [block[middle:] for block in blocks]]
+    arrived = {1: [blocks[0], blocks[1], *notes]}
     for step in range(2, quarter + 1):
-        blocks = both(*blocks)
+        plain = both(*halves[0])
+        other = both(*halves[1])
+        halves = [plain, other]
         notes = [
             send(note[: height(step)], sign * step)
             for note, sign in ((right_note, 1), (left_note, -1))
         ]
-        arrived[step] = blocks + notes
-    message = jax.ShapeDtypeStruct((block_rows + height(quarter + 1), features), embeddings.dtype)
-    right, left = pl.pallas_call(
+        arrived[step] = plain + other + notes
+    message = jax.ShapeDtypeStruct((middle + height(quarter + 1), features), embeddings.dtype)
+    noted = pl.pallas_call(
         functools.partial(join_body, pad),
         out_shape=[message, message],
         in_specs=[VMEM] * 4,
@@ -439,30 +443,35 @@
         compiler_params=compiler_params(4),
         cost_estimate=cost(0.3),
         name="join",
-    )(*blocks, *notes)
+    )(*halves[1], *notes)
+    plain = halves[0]
     for step in range(quarter + 1, half):
-        keep = block_rows + height(step)
-        right, left = arrived[step] = both(right[:keep], left[:keep])
-    middle = pad + block_rows // 2
-    arrived[half] = both(right[:middle], left[middle : pad + block_rows])
+        plain = both(*plain)
+        noted = both(*(note[: middle + height(step)] for note in noted))
+        arrived[step] = plain + noted
+    arrived[half] = [send(plain[1], -1), send(noted[0][: middle + pad], 1)]
+
+    def front_of(step, side):
+        if step == half:
+            return 1
+        return side + 4 if 1 < step <= quarter else side + 2
 
     def spot_of(step, side, distance):
         row, column = list_spot(groups, distance, block_rows, pad)
+        return front_of(step, side), row + (middle if row and step > quarter else 0), column
+
+    def block_of(step, side):
+        if step == 1:
+            return [(side, 0, block_rows)]
         if step <= quarter:
-            return side + 2, row, column
-        return side, row + (block_rows if row else 0), column
-
-    def block_of(step, side):
-        start = 0 if step <= quarter else pad
-        return [(side, start, start + block_rows)]
-
-    def front_of(step, side):
-        return side + 2 if step <= quarter else side
+            return [(side, 0, middle), (side + 2, 0, middle)]
+        if step == half:
+            return [(0, 0, middle), (1, pad, pad + middle)]
+        return [(side, 0, middle), (side + 2, pad, pad + middle)]
 
     def tiles_of(step):
         if step == half:
-            pieces = [(0, pad, middle), (1, 0, block_rows // 2)]
-            return [(place_of[half], pieces, 0, spot_of(step, 0, half))]
+            return [(place_of[half], block_of(step, 0), front_of(step, 0), spot_of(step, 0, half))]
         return [
             (place_of[sign * step], block_of(step, side), front_of(step, side), spot_of(step, side, step))
             for side, sign in ((0, -1), (1, 1))
@@ -499,18 +508,17 @@
             sources, pairs = list(arrived[step]), []
             for distance in range(quarter + 1, half + 1):
                 lower = distance - quarter
-                at, front, factor = 0, 2, 1.0
+                base_at, factor = 0, 1.0
                 if lower != quarter:
-                    at, front, factor = len(sources), len(sources) + 1, 2.0
-                    sources += [arrived[lower][0], arrived[lower][2]]
-                there = (front,) + spot_of(step, 0, distance)[1:]
+                    base_at, factor = len(sources), 2.0
+                    sources += arrived[lower]
                 pairs.append(
                     (
-                        block_of(step, at),
-                        front,
+                        [(at + base_at, low, high) for at, low, high in block_of(lower, 0)],
+                        front_of(lower, 0) + base_at,
                         block_of(step, 1),
-                        3,
-                        there,
+                        front_of(step, 1),
+                        (front_of(lower, 0) + base_at, *spot_of(lower, 0, distance)[1:]),
                         spot_of(step, 1, distance),
                         factor,
                     )
@@ -525,7 +533,7 @@
                 ],
                 1.8,
             )
-            operands = [kernels, counts] + arrived[step][:2]
+            operands = [kernels, counts] + arrived[step]
             state = call(
                 functools.partial(pull_body, tiles),
                 operands + list(state[:2]),

time: 50.5 us -> 49.7 us (0.984)
  waiting for transfers between devices: 16.8 us -> 11.3 us
  starting transfers between devices: 23.9 us -> 28.7 us
    ppermute x16 -> x20, waiting for transfers between devices: 13.6 us -> 8.05 us  [send(): return lax.ppermute(value, 'wide', shift_pairs(groups, offset))]
    ppermute x16 -> x20, starting transfers between devices: 22.3 us -> 27.1 us  [send(): return lax.ppermute(value, 'wide', shift_pairs(groups, offset))]
  transfers between devices with their start and end apart: 18 -> 22, of which waited for: 8 -> 8; matrix products, arithmetic and copies ran while one was open for 0% -> 0% of each run, Pallas kernels for 15% -> 12%
where the time goes in v2:
time: 49.7 us; the launch traced here: 49.6 us
  starting transfers between devices  28.7 us (58%)
  waiting for transfers between devices  11.3 us (23%)
  Pallas kernels  8.84 us (18%)
  between operations  0.77 us (2%)
    ppermute x20, starting transfers between devices, send(): return lax.ppermute(value, 'wide', shift_pairs(groups, offset))  27.1 us
    ppermute x20, waiting for transfers between devices, send(): return lax.ppermute(value, 'wide', shift_pairs(groups, offset))  8.05 us
    pallas_call x6, Pallas kernels, call(): pl.pallas_call(body, out_shape=shapes, in_specs=[VMEM] * len(operands), o...  6.61 us
    ppermute x2, waiting for transfers between devices, column_step(): lax.ppermute(window, 'narrow', [(k, k ^ bit) for k in range(columns)])  3.2 us
    ppermute x2, starting transfers between devices, column_step(): lax.ppermute(window, 'narrow', [(k, k ^ bit) for k in range(columns)])  1.59 us
    pallas_call x1, Pallas kernels, column_step(): pl.pallas_call(functools.partial(prepare_body, groups, offsets), out_shap...  1.32 us
  transfers between devices with their start and end apart: 22, of which 8 were waited for; matrix products, arithmetic and copies ran while one was open for 0% of the time, Pallas kernels for 12%

profile of v2, /device:TPU:0, one launch (start us, length us, event | category | flops | bytes accessed | tf_op | source)
XLA Modules:
  0.0 49.6 jit_solution(2223959852986798995)
XLA Ops:
  0.6 3.1 %collective-permute-start = (bf16[256,512]{1,0:T(8,128)(2,1)}, bf16[256,512]{1,0:T(8,128)(2,1)S(1)}, u32[]{:S(2)}, u32[]{:S(2)}) collective-permute-start(bf16[256,512]{1,0:T(8,128)(2,1)} %refs_3_.1), channel_id=1, source_target_pairs={{0,8},{8,16},{16,24},{24,28},{28,20},{20,12},{12,4},{4,0},{1,9},{9... | collective-permute-start | bytes 786440 | tf_op jit(solution)/shard_map/ppermute | solution.py:385
  3.7 0.0 collective-permute-start.1
  3.7 1.3 %prepare.1 = (bf16[32,512]{1,0:T(8,128)(2,1)S(1)}, bf16[32,512]{1,0:T(8,128)(2,1)S(1)}, bf16[7,16,256]{2,1,0:T(8,128)(2,1)S(1)}, f32[1,128]{1,0:T(1,128)S(1)}, bf16[256,512]{1,0:T(8,128)(2,1)S(1)}) custom-call(s32[1,7]{1,0:T(1,128)} %refs_0_.1, s32[1,7]{1,0:T(1,128)} %refs_1_.1, s32[7,15,256]{2,1,0:T(8,128)} %refs_2_.1, bf16[256,512]{1,0:T(8,128)(2,1)} %refs_3_.1), custom_call_target="tpu_custom_call" | custom-call | flops 1200000000 | bytes 3000000 | tf_op jit(solution)/shard_map/prepare/pallas_call | solution.py:394
  5.1 2.1 %collective-permute-start.2 = (bf16[32,512]{1,0:T(8,128)(2,1)S(1)}, bf16[32,512]{1,0:T(8,128)(2,1)S(1)}, u32[]{:S(2)}, u32[]{:S(2)}) collective-permute-start(bf16[32,512]{1,0:T(8,128)(2,1)S(1)} %get-tuple-element.24.refs_1_), channel_id=1, source_target_pairs={{0,8},{8,16},{16,24},{24,28},{28,20},{20,12},{12,4},{4,0},{1,9},{9... | collective-permute-start | bytes 98312 | tf_op jit(solution)/shard_map/ppermute | solution.py:385
  7.2 2.6 %collective-permute-start.8 = (bf16[32,512]{1,0:T(8,128)(2,1)S(1)}, bf16[32,512]{1,0:T(8,128)(2,1)S(1)}, u32[]{:S(2)}, u32[]{:S(2)}) collective-permute-start(bf16[32,512]{1,0:T(8,128)(2,1)S(1)} %get-tuple-element.24.refs_1_), channel_id=1, source_target_pairs={{0,16},{8,24},{16,28},{24,20},{28,12},{20,4},{12,0},{4,8},{1,17},{... | collective-permute-start | bytes 98312 | tf_op jit(solution)/shard_map/ppermute | solution.py:385
  9.7 0.5 collective-permute-start.3
  10.2 0.9 %own_counts.1.refs_2_ = bf16[7,256,256]{2,1,0:T(8,128)(2,1)S(1)} custom-call(bf16[7,16,256]{2,1,0:T(8,128)(2,1)S(1)} %get-tuple-element.25.own), custom_call_target="tpu_custom_call" | custom-call | flops 800000000 | bytes 2000000 | tf_op jit(solution)/shard_map/own_counts/pallas_call | solution.py:416
  11.1 0.0 collective-permute-done.refs_3_.refs_11_
  11.1 2.6 %collective-permute-start.9 = (bf16[32,512]{1,0:T(8,128)(2,1)S(1)}, bf16[32,512]{1,0:T(8,128)(2,1)S(1)}, u32[]{:S(2)}, u32[]{:S(2)}) collective-permute-start(bf16[32,512]{1,0:T(8,128)(2,1)S(1)} %get-tuple-element.27), channel_id=1, source_target_pairs={{0,12},{8,4},{16,0},{24,8},{28,16},{20,24},{12,28},{4,20},{1,13},{... | collective-permute-start | bytes 98312 | tf_op jit(solution)/shard_map/ppermute | solution.py:385
  13.8 0.0 collective-permute-done.1.refs_4_.refs_12_
  13.8 0.5 %collective-permute-start.4 = (bf16[128,512]{1,0:T(8,128)(2,1)S(1)}, bf16[128,512]{1,0:T(8,128)(2,1)S(1)}, u32[]{:S(2)}, u32[]{:S(2)}) collective-permute-start(bf16[128,512]{1,0:T(8,128)(2,1)S(1)} %get-tuple-element.47), channel_id=1, source_target_pairs={{0,8},{8,16},{16,24},{24,28},{28,20},{20,12},{12,4},{4,0},{1,9},{9... | collective-permute-start | bytes 393224 | tf_op jit(solution)/shard_map/ppermute | solution.py:385
  14.3 0.0 collective-permute-done.2.refs_5_.refs_13_
  14.3 1.6 %collective-permute-start.5 = (bf16[128,512]{1,0:T(8,128)(2,1)S(1)}, bf16[128,512]{1,0:T(8,128)(2,1)S(1)}, u32[]{:S(2)}, u32[]{:S(2)}) collective-permute-start(bf16[128,512]{1,0:T(8,128)(2,1)S(1)} %get-tuple-element.45), channel_id=1, source_target_pairs={{0,4},{8,0},{16,8},{24,16},{28,24},{20,28},{12,20},{4,12},{1,5},{9... | collective-permute-start | bytes 393224 | tf_op jit(solution)/shard_map/ppermute | solution.py:385
  15.9 0.0 collective-permute-done.3.refs_6_.refs_14_
  15.9 0.5 collective-permute-start.6
  16.4 0.0 collective-permute-done.8.refs_9_.right_lists.refs_6_
  16.4 1.6 %collective-permute-start.7 = (bf16[128,512]{1,0:T(8,128)(2,1)S(1)}, bf16[128,512]{1,0:T(8,128)(2,1)S(1)}, u32[]{:S(2)}, u32[]{:S(2)}) collective-permute-start(bf16[128,512]{1,0:T(8,128)(2,1)S(1)} %get-tuple-element.44), channel_id=1, source_target_pairs={{0,4},{8,0},{16,8},{24,16},{28,24},{20,28},{12,20},{4,12},{1,5},{9... | collective-permute-start | bytes 393224 | tf_op jit(solution)/shard_map/ppermute | solution.py:385
  18.0 1.3 %shard_map.59 = (f32[2,256,512]{2,1,0:T(8,128)S(1)}, f32[2,256,1]{2,1,0:T(8,128)S(1)}, f32[2,8,256]{2,1,0:T(8,128)S(1)}) custom-call(bf16[256,512]{1,0:T(8,128)(2,1)S(1)} %get-tuple-element.23.refs_0_.refs_3_, bf16[32,512]{1,0:T(8,128)(2,1)S(1)} %get-tuple-element.24.refs_1_, bf16[7,256,256]{2,1,0:T(8,128)(2,1)S(1)} %own_counts.1.refs_2_, ...), custom_call_target="tpu_custom_call" | custom-call | flops 1600000000 | bytes 4000000 | tf_op jit(solution)/shard_map/pallas_call | solution.py:481
  19.2 0.0 collective-permute-done.9.refs_10_.left_lists.refs_7_
  19.2 0.0 collective-permute-done.4.refs_5_.refs_2_
  19.2 0.2 collective-permute-done.5.refs_6_.refs_3_
  19.5 1.4 %collective-permute-done.6.refs_7_.right_block.refs_4_ = bf16[128,512]{1,0:T(8,128)(2,1)S(1)} collective-permute-done((bf16[128,512]{1,0:T(8,128)(2,1)S(1)}, bf16[128,512]{1,0:T(8,128)(2,1)S(1)}, u32[]{:S(2)}, u32[]{:S(2)}) %collective-permute-start.6) | collective-permute-done | bytes 131104 | tf_op jit(solution)/shard_map/ppermute | solution.py:385
  20.9 0.5 collective-permute-done.7.refs_8_.left_block.refs_5_
  21.4 1.6 %shard_map.60 = (f32[1,128]{1,0:T(1,128)S(1)}, f32[2,256,256]{2,1,0:T(8,128)S(1)}, bf16[2,256,256]{2,1,0:T(8,128)(2,1)S(1)}) custom-call(bf16[256,512]{1,0:T(8,128)(2,1)S(1)} %get-tuple-element.23.refs_0_.refs_3_, bf16[32,512]{1,0:T(8,128)(2,1)S(1)} %get-tuple-element.24.refs_1_, bf16[7,256,256]{2,1,0:T(8,128)(2,1)S(1)} %own_counts.1.refs_2_, ...), custom_call_target="tpu_custom_call" | custom-call | flops 1440000000 | bytes 3600000 | tf_op jit(solution)/shard_map/pallas_call | solution.py:481
  22.9 0.1 collective-permute-start.10
  23.0 1.1 %collective-permute-done.10 = f32[1,128]{1,0:T(1,128)S(1)} collective-permute-done((f32[1,128]{1,0:T(1,128)S(1)}, f32[1,128]{1,0:T(1,128)S(1)}, u32[]{:S(2)}, u32[]{:S(2)}) %collective-permute-start.10) | collective-permute-done | bytes 544 | tf_op jit(solution)/shard_map/ppermute | solution.py:562
  24.2 1.5 %collective-permute-start.11 = (f32[1,128]{1,0:T(1,128)S(1)}, f32[1,128]{1,0:T(1,128)S(1)}, u32[]{:S(2)}, u32[]{:S(2)}) collective-permute-start(f32[1,128]{1,0:T(1,128)S(1)} %add.6), channel_id=1, source_target_pairs={{0,2},{1,3},{2,0},{3,1},{4,6},{5,7},{6,4},{7,5},{8,10},{9,11},{10,... | collective-permute-start | bytes 1544 | tf_op jit(solution)/shard_map/ppermute | solution.py:562
  25.7 2.1 %collective-permute-done.11 = f32[1,128]{1,0:T(1,128)S(1)} collective-permute-done((f32[1,128]{1,0:T(1,128)S(1)}, f32[1,128]{1,0:T(1,128)S(1)}, u32[]{:S(2)}, u32[]{:S(2)}) %collective-permute-start.11) | collective-permute-done | bytes 544 | tf_op jit(solution)/shard_map/ppermute | solution.py:562
  27.7 1.7 %collective-permute-start.12 = (f32[1,128]{1,0:T(1,128)S(1)}, f32[1,128]{1,0:T(1,128)S(1)}, u32[]{:S(2)}, u32[]{:S(2)}) collective-permute-start(f32[1,128]{1,0:T(1,128)S(1)} %add.7), channel_id=1, source_target_pairs={{0,8},{8,16},{16,24},{24,28},{28,20},{20,12},{12,4},{4,0},{1,9},{9... | collective-permute-start | bytes 1544 | tf_op jit(solution)/shard_map/ppermute | solution.py:385
  29.4 0.8 %collective-permute-start.18 = (bf16[144,512]{1,0:T(8,128)(2,1)S(1)}, bf16[144,512]{1,0:T(8,128)(2,1)S(1)}, u32[]{:S(2)}, u32[]{:S(2)}) collective-permute-start(bf16[144,512]{1,0:T(8,128)(2,1)S(1)} %get-tuple-element.30), channel_id=1, source_target_pairs={{0,8},{8,16},{16,24},{24,28},{28,20},{20,12},{12,4},{4,0},{1,9},{9... | collective-permute-start | bytes 442376 | tf_op jit(solution)/shard_map/ppermute | solution.py:385
  30.2 1.2 %collective-permute-start.21 = (bf16[144,512]{1,0:T(8,128)(2,1)S(1)}, bf16[144,512]{1,0:T(8,128)(2,1)S(1)}, u32[]{:S(2)}, u32[]{:S(2)}) collective-permute-start(bf16[144,512]{1,0:T(8,128)(2,1)S(1)} %get-tuple-element.31), channel_id=1, source_target_pairs={{0,4},{8,0},{16,8},{24,16},{28,24},{20,28},{12,20},{4,12},{1,5},{9... | collective-permute-start | bytes 442376 | tf_op jit(solution)/shard_map/ppermute | solution.py:385
  31.5 0.4 collective-permute-start.16
  31.9 1.7 %collective-permute-start.20 = (bf16[128,512]{1,0:T(8,128)(2,1)S(1)}, bf16[128,512]{1,0:T(8,128)(2,1)S(1)}, u32[]{:S(2)}, u32[]{:S(2)}) collective-permute-start(bf16[128,512]{1,0:T(8,128)(2,1)S(1)} %collective-permute-done.4.refs_5_.refs_2_), channel_id=1, source_target_pairs={{0,8},{8,16},{16,24},{24,28},{28,20},{20,12},{12,4},{4,0},{1,9},{9... | collective-permute-start | bytes 393224 | tf_op jit(solution)/shard_map/ppermute | solution.py:385
  33.5 0.0 collective-permute-done.12
  33.5 0.4 collective-permute-start.13
  33.9 0.6 %shard_map.61 = (f32[2,256,512]{2,1,0:T(8,128)S(1)}, f32[2,256,1]{2,1,0:T(8,128)S(1)}) custom-call(f32[2,256,256]{2,1,0:T(8,128)S(1)} %get-tuple-element.32.refs_0_, bf16[2,256,256]{2,1,0:T(8,128)(2,1)S(1)} %get-tuple-element.33.refs_1_, bf16[128,512]{1,0:T(8,128)(2,1)S(1)} %collective-permute-done.4.refs_5_.refs_2_, ...), custom_call_target="tpu_custom_call", output_to_operand_aliasing={{0}: (8, {}), {1}: (9, {})} | custom-call | flops 1200000000 | bytes 3000000 | tf_op jit(solution)/shard_map/pallas_call | solution.py:481
  34.5 2.8 %collective-permute-done.13 = f32[1,128]{1,0:T(1,128)S(1)} collective-permute-done((f32[1,128]{1,0:T(1,128)S(1)}, f32[1,128]{1,0:T(1,128)S(1)}, u32[]{:S(2)}, u32[]{:S(2)}) %collective-permute-start.13) | collective-permute-done | bytes 544 | tf_op jit(solution)/shard_map/ppermute | solution.py:385
  37.4 2.1 %collective-permute-start.14 = (f32[3,128]{1,0:T(4,128)S(1)}, f32[3,128]{1,0:T(4,128)S(1)}, u32[]{:S(2)}, u32[]{:S(2)}) collective-permute-start(f32[3,128]{1,0:T(4,128)S(1)} %pad_maximum_fusion.refs_0_), channel_id=1, source_target_pairs={{0,20},{8,12},{16,4},{24,0},{28,8},{20,16},{12,24},{4,28},{1,21},{... | collective-permute-start | bytes 4616 | tf_op jit(solution)/shard_map/ppermute | solution.py:385
  39.5 0.0 collective-permute-done.16.refs_4_
  39.5 1.7 %collective-permute-start.15 = (f32[3,128]{1,0:T(4,128)S(1)}, f32[3,128]{1,0:T(4,128)S(1)}, u32[]{:S(2)}, u32[]{:S(2)}) collective-permute-start(f32[3,128]{1,0:T(4,128)S(1)} %pad_maximum_fusion.refs_0_), channel_id=1, source_target_pairs={{0,24},{8,28},{16,20},{24,12},{28,4},{20,0},{12,8},{4,16},{1,25},{... | collective-permute-start | bytes 4616 | tf_op jit(solution)/shard_map/ppermute | solution.py:385
  41.3 0.0 collective-permute-done.20.refs_3_
  41.3 1.2 %collective-permute-start.17 = (bf16[128,512]{1,0:T(8,128)(2,1)S(1)}, bf16[128,512]{1,0:T(8,128)(2,1)S(1)}, u32[]{:S(2)}, u32[]{:S(2)}) collective-permute-start(bf16[128,512]{1,0:T(8,128)(2,1)S(1)} %collective-permute-done.16.refs_4_), channel_id=1, source_target_pairs={{0,4},{8,0},{16,8},{24,16},{28,24},{20,28},{12,20},{4,12},{1,5},{9... | collective-permute-start | bytes 393224 | tf_op jit(solution)/shard_map/ppermute | solution.py:385
  42.5 0.0 collective-permute-done.18.refs_5_
  42.5 0.8 %collective-permute-start.19 = (bf16[144,512]{1,0:T(8,128)(2,1)S(1)}, bf16[144,512]{1,0:T(8,128)(2,1)S(1)}, u32[]{:S(2)}, u32[]{:S(2)}) collective-permute-start(bf16[144,512]{1,0:T(8,128)(2,1)S(1)} %collective-permute-done.18.refs_5_), channel_id=1, source_target_pairs={{0,8},{8,16},{16,24},{24,28},{28,20},{20,12},{12,4},{4,0},{1,9},{9... | collective-permute-start | bytes 442376 | tf_op jit(solution)/shard_map/ppermute | solution.py:385
  43.3 0.0 collective-permute-done.21.refs_6_
  43.3 1.3 %shard_map.62 = (f32[2,256,512]{2,1,0:T(8,128)S(1)}, f32[2,256,1]{2,1,0:T(8,128)S(1)}) custom-call(bf16[256,512]{1,0:T(8,128)(2,1)S(1)} %get-tuple-element.23.refs_0_.refs_3_, bf16[32,512]{1,0:T(8,128)(2,1)S(1)} %get-tuple-element.24.refs_1_, bf16[7,256,256]{2,1,0:T(8,128)(2,1)S(1)} %own_counts.1.refs_2_, ...), custom_call_target="tpu_custom_call", output_to_operand_aliasing={{0}: (7, {}), {1}: (8, {})} | custom-call | flops 1600000000 | bytes 4000000 | tf_op jit(solution)/shard_map/pallas_call | solution.py:481
  44.6 1.7 %collective-permute-done.17.refs_3_ = bf16[128,512]{1,0:T(8,128)(2,1)S(1)} collective-permute-done((bf16[128,512]{1,0:T(8,128)(2,1)S(1)}, bf16[128,512]{1,0:T(8,128)(2,1)S(1)}, u32[]{:S(2)}, u32[]{:S(2)}) %collective-permute-start.17) | collective-permute-done | bytes 131104 | tf_op jit(solution)/shard_map/ppermute | solution.py:385
  46.2 1.4 %collective-permute-done.19.refs_4_ = bf16[144,512]{1,0:T(8,128)(2,1)S(1)} collective-permute-done((bf16[144,512]{1,0:T(8,128)(2,1)S(1)}, bf16[144,512]{1,0:T(8,128)(2,1)S(1)}, u32[]{:S(2)}, u32[]{:S(2)}) %collective-permute-start.19) | collective-permute-done | bytes 147488 | tf_op jit(solution)/shard_map/ppermute | solution.py:385
  47.6 0.8 %shard_map.63 = (f32[2,256,512]{2,1,0:T(8,128)S(1)}, f32[2,256,1]{2,1,0:T(8,128)S(1)}) custom-call(bf16[256,512]{1,0:T(8,128)(2,1)S(1)} %get-tuple-element.23.refs_0_.refs_3_, bf16[32,512]{1,0:T(8,128)(2,1)S(1)} %get-tuple-element.24.refs_1_, bf16[7,256,256]{2,1,0:T(8,128)(2,1)S(1)} %own_counts.1.refs_2_, ...), custom_call_target="tpu_custom_call", output_to_operand_aliasing={{0}: (5, {}), {1}: (6, {})} | custom-call | flops 1600000000 | bytes 4000000 | tf_op jit(solution)/shard_map/pallas_call | solution.py:481
  48.4 0.0 collective-permute-done.14.refs_1_
  48.4 0.0 collective-permute-done.15.refs_2_
  48.5 1.1 %shard_map.64 = (f32[256,512]{1,0:T(8,128)}, f32[1,1]{1,0:T(1,128)}) custom-call(f32[3,128]{1,0:T(4,128)S(1)} %pad_maximum_fusion.refs_0_, f32[3,128]{1,0:T(4,128)S(1)} %collective-permute-done.14.refs_1_, f32[3,128]{1,0:T(4,128)S(1)} %collective-permute-done.15.refs_2_, bf16[256,512]{1,0:T(8,128)(2,1)S(1)} %get-tuple-element.23.refs_0_.refs_3_, ...), custom_call_target="tpu_custom_call" | custom-call | flops 800000000 | bytes 2000000 | tf_op jit(solution)/shard_map/pallas_call | solution.py:481
  (6 shorter events, 0.1 us)
Async XLA Ops:
  0.6 10.5 %collective-permute-start = (bf16[256,512]{1,0:T(8,128)(2,1)}, bf16[256,512]{1,0:T(8,128)(2,1)S(1)}, u32[]{:S(2)}, u32[]{:S(2)}) collective-permute-start(bf16[256,512]{1,0:T(8,128)(2,1)} %refs_3_.1), channel_id=1, source_target_pairs={{0,8},{8,16},{16,24},{24,28},{28,20},{20,12},{12,4},{4,0},{1,9},{9... | collective-permute-start | bytes 786440 | tf_op jit(solution)/shard_map/ppermute | solution.py:385
  3.7 10.0 %collective-permute-start.1 = (bf16[256,512]{1,0:T(8,128)(2,1)}, bf16[256,512]{1,0:T(8,128)(2,1)S(1)}, u32[]{:S(2)}, u32[]{:S(2)}) collective-permute-start(bf16[256,512]{1,0:T(8,128)(2,1)} %refs_3_.1), channel_id=1, source_target_pairs={{0,4},{8,0},{16,8},{24,16},{28,24},{20,28},{12,20},{4,12},{1,5},{9... | collective-permute-start | bytes 786440 | tf_op jit(solution)/shard_map/ppermute | solution.py:385
  5.1 9.2 %collective-permute-start.2 = (bf16[32,512]{1,0:T(8,128)(2,1)S(1)}, bf16[32,512]{1,0:T(8,128)(2,1)S(1)}, u32[]{:S(2)}, u32[]{:S(2)}) collective-permute-start(bf16[32,512]{1,0:T(8,128)(2,1)S(1)} %get-tuple-element.24.refs_1_), channel_id=1, source_target_pairs={{0,8},{8,16},{16,24},{24,28},{28,20},{20,12},{12,4},{4,0},{1,9},{9... | collective-permute-start | bytes 98312 | tf_op jit(solution)/shard_map/ppermute | solution.py:385
  7.2 9.2 %collective-permute-start.8 = (bf16[32,512]{1,0:T(8,128)(2,1)S(1)}, bf16[32,512]{1,0:T(8,128)(2,1)S(1)}, u32[]{:S(2)}, u32[]{:S(2)}) collective-permute-start(bf16[32,512]{1,0:T(8,128)(2,1)S(1)} %get-tuple-element.24.refs_1_), channel_id=1, source_target_pairs={{0,16},{8,24},{16,28},{24,20},{28,12},{20,4},{12,0},{4,8},{1,17},{... | collective-permute-start | bytes 98312 | tf_op jit(solution)/shard_map/ppermute | solution.py:385
  9.7 6.2 %collective-permute-start.3 = (bf16[32,512]{1,0:T(8,128)(2,1)S(1)}, bf16[32,512]{1,0:T(8,128)(2,1)S(1)}, u32[]{:S(2)}, u32[]{:S(2)}) collective-permute-start(bf16[32,512]{1,0:T(8,128)(2,1)S(1)} %get-tuple-element.27), channel_id=1, source_target_pairs={{0,4},{8,0},{16,8},{24,16},{28,24},{20,28},{12,20},{4,12},{1,5},{9... | collective-permute-start | bytes 98312 | tf_op jit(solution)/shard_map/ppermute | solution.py:385
  11.1 8.1 %collective-permute-start.9 = (bf16[32,512]{1,0:T(8,128)(2,1)S(1)}, bf16[32,512]{1,0:T(8,128)(2,1)S(1)}, u32[]{:S(2)}, u32[]{:S(2)}) collective-permute-start(bf16[32,512]{1,0:T(8,128)(2,1)S(1)} %get-tuple-element.27), channel_id=1, source_target_pairs={{0,12},{8,4},{16,0},{24,8},{28,16},{20,24},{12,28},{4,20},{1,13},{... | collective-permute-start | bytes 98312 | tf_op jit(solution)/shard_map/ppermute | solution.py:385
  13.8 5.5 %collective-permute-start.4 = (bf16[128,512]{1,0:T(8,128)(2,1)S(1)}, bf16[128,512]{1,0:T(8,128)(2,1)S(1)}, u32[]{:S(2)}, u32[]{:S(2)}) collective-permute-start(bf16[128,512]{1,0:T(8,128)(2,1)S(1)} %get-tuple-element.47), channel_id=1, source_target_pairs={{0,8},{8,16},{16,24},{24,28},{28,20},{20,12},{12,4},{4,0},{1,9},{9... | collective-permute-start | bytes 393224 | tf_op jit(solution)/shard_map/ppermute | solution.py:385
  14.3 5.2 %collective-permute-start.5 = (bf16[128,512]{1,0:T(8,128)(2,1)S(1)}, bf16[128,512]{1,0:T(8,128)(2,1)S(1)}, u32[]{:S(2)}, u32[]{:S(2)}) collective-permute-start(bf16[128,512]{1,0:T(8,128)(2,1)S(1)} %get-tuple-element.45), channel_id=1, source_target_pairs={{0,4},{8,0},{16,8},{24,16},{28,24},{20,28},{12,20},{4,12},{1,5},{9... | collective-permute-start | bytes 393224 | tf_op jit(solution)/shard_map/ppermute | solution.py:385
  15.9 5.0 %collective-permute-start.6 = (bf16[128,512]{1,0:T(8,128)(2,1)S(1)}, bf16[128,512]{1,0:T(8,128)(2,1)S(1)}, u32[]{:S(2)}, u32[]{:S(2)}) collective-permute-start(bf16[128,512]{1,0:T(8,128)(2,1)S(1)} %get-tuple-element.46), channel_id=1, source_target_pairs={{0,8},{8,16},{16,24},{24,28},{28,20},{20,12},{12,4},{4,0},{1,9},{9... | collective-permute-start | bytes 393224 | tf_op jit(solution)/shard_map/ppermute | solution.py:385
  16.4 5.0 %collective-permute-start.7 = (bf16[128,512]{1,0:T(8,128)(2,1)S(1)}, bf16[128,512]{1,0:T(8,128)(2,1)S(1)}, u32[]{:S(2)}, u32[]{:S(2)}) collective-permute-start(bf16[128,512]{1,0:T(8,128)(2,1)S(1)} %get-tuple-element.44), channel_id=1, source_target_pairs={{0,4},{8,0},{16,8},{24,16},{28,24},{20,28},{12,20},{4,12},{1,5},{9... | collective-permute-start | bytes 393224 | tf_op jit(solution)/shard_map/ppermute | solution.py:385
  22.9 1.2 %collective-permute-start.10 = (f32[1,128]{1,0:T(1,128)S(1)}, f32[1,128]{1,0:T(1,128)S(1)}, u32[]{:S(2)}, u32[]{:S(2)}) collective-permute-start(f32[1,128]{1,0:T(1,128)S(1)} %get-tuple-element.29), channel_id=1, source_target_pairs={{0,1},{1,0},{2,3},{3,2},{4,5},{5,4},{6,7},{7,6},{8,9},{9,8},{10,11... | collective-permute-start | bytes 1544 | tf_op jit(solution)/shard_map/ppermute | solution.py:562
  24.2 3.6 %collective-permute-start.11 = (f32[1,128]{1,0:T(1,128)S(1)}, f32[1,128]{1,0:T(1,128)S(1)}, u32[]{:S(2)}, u32[]{:S(2)}) collective-permute-start(f32[1,128]{1,0:T(1,128)S(1)} %add.6), channel_id=1, source_target_pairs={{0,2},{1,3},{2,0},{3,1},{4,6},{5,7},{6,4},{7,5},{8,10},{9,11},{10,... | collective-permute-start | bytes 1544 | tf_op jit(solution)/shard_map/ppermute | solution.py:562
  27.7 5.8 %collective-permute-start.12 = (f32[1,128]{1,0:T(1,128)S(1)}, f32[1,128]{1,0:T(1,128)S(1)}, u32[]{:S(2)}, u32[]{:S(2)}) collective-permute-start(f32[1,128]{1,0:T(1,128)S(1)} %add.7), channel_id=1, source_target_pairs={{0,8},{8,16},{16,24},{24,28},{28,20},{20,12},{12,4},{4,0},{1,9},{9... | collective-permute-start | bytes 1544 | tf_op jit(solution)/shard_map/ppermute | solution.py:385
  29.4 13.1 %collective-permute-start.18 = (bf16[144,512]{1,0:T(8,128)(2,1)S(1)}, bf16[144,512]{1,0:T(8,128)(2,1)S(1)}, u32[]{:S(2)}, u32[]{:S(2)}) collective-permute-start(bf16[144,512]{1,0:T(8,128)(2,1)S(1)} %get-tuple-element.30), channel_id=1, source_target_pairs={{0,8},{8,16},{16,24},{24,28},{28,20},{20,12},{12,4},{4,0},{1,9},{9... | collective-permute-start | bytes 442376 | tf_op jit(solution)/shard_map/ppermute | solution.py:385
  30.2 13.0 %collective-permute-start.21 = (bf16[144,512]{1,0:T(8,128)(2,1)S(1)}, bf16[144,512]{1,0:T(8,128)(2,1)S(1)}, u32[]{:S(2)}, u32[]{:S(2)}) collective-permute-start(bf16[144,512]{1,0:T(8,128)(2,1)S(1)} %get-tuple-element.31), channel_id=1, source_target_pairs={{0,4},{8,0},{16,8},{24,16},{28,24},{20,28},{12,20},{4,12},{1,5},{9... | collective-permute-start | bytes 442376 | tf_op jit(solution)/shard_map/ppermute | solution.py:385
  31.5 8.0 %collective-permute-start.16 = (bf16[128,512]{1,0:T(8,128)(2,1)S(1)}, bf16[128,512]{1,0:T(8,128)(2,1)S(1)}, u32[]{:S(2)}, u32[]{:S(2)}) collective-permute-start(bf16[128,512]{1,0:T(8,128)(2,1)S(1)} %collective-permute-done.5.refs_6_.refs_3_), channel_id=1, source_target_pairs={{0,4},{8,0},{16,8},{24,16},{28,24},{20,28},{12,20},{4,12},{1,5},{9... | collective-permute-start | bytes 393224 | tf_op jit(solution)/shard_map/ppermute | solution.py:385
  31.9 9.4 %collective-permute-start.20 = (bf16[128,512]{1,0:T(8,128)(2,1)S(1)}, bf16[128,512]{1,0:T(8,128)(2,1)S(1)}, u32[]{:S(2)}, u32[]{:S(2)}) collective-permute-start(bf16[128,512]{1,0:T(8,128)(2,1)S(1)} %collective-permute-done.4.refs_5_.refs_2_), channel_id=1, source_target_pairs={{0,8},{8,16},{16,24},{24,28},{28,20},{20,12},{12,4},{4,0},{1,9},{9... | collective-permute-start | bytes 393224 | tf_op jit(solution)/shard_map/ppermute | solution.py:385
  33.5 3.8 %collective-permute-start.13 = (f32[1,128]{1,0:T(1,128)S(1)}, f32[1,128]{1,0:T(1,128)S(1)}, u32[]{:S(2)}, u32[]{:S(2)}) collective-permute-start(f32[1,128]{1,0:T(1,128)S(1)} %add.7), channel_id=1, source_target_pairs={{0,4},{8,0},{16,8},{24,16},{28,24},{20,28},{12,20},{4,12},{1,5},{9... | collective-permute-start | bytes 1544 | tf_op jit(solution)/shard_map/ppermute | solution.py:385
  37.4 11.1 %collective-permute-start.14 = (f32[3,128]{1,0:T(4,128)S(1)}, f32[3,128]{1,0:T(4,128)S(1)}, u32[]{:S(2)}, u32[]{:S(2)}) collective-permute-start(f32[3,128]{1,0:T(4,128)S(1)} %pad_maximum_fusion.refs_0_), channel_id=1, source_target_pairs={{0,20},{8,12},{16,4},{24,0},{28,8},{20,16},{12,24},{4,28},{1,21},{... | collective-permute-start | bytes 4616 | tf_op jit(solution)/shard_map/ppermute | solution.py:385
  39.5 8.9 %collective-permute-start.15 = (f32[3,128]{1,0:T(4,128)S(1)}, f32[3,128]{1,0:T(4,128)S(1)}, u32[]{:S(2)}, u32[]{:S(2)}) collective-permute-start(f32[3,128]{1,0:T(4,128)S(1)} %pad_maximum_fusion.refs_0_), channel_id=1, source_target_pairs={{0,24},{8,28},{16,20},{24,12},{28,4},{20,0},{12,8},{4,16},{1,25},{... | collective-permute-start | bytes 4616 | tf_op jit(solution)/shard_map/ppermute | solution.py:385
  41.3 5.0 %collective-permute-start.17 = (bf16[128,512]{1,0:T(8,128)(2,1)S(1)}, bf16[128,512]{1,0:T(8,128)(2,1)S(1)}, u32[]{:S(2)}, u32[]{:S(2)}) collective-permute-start(bf16[128,512]{1,0:T(8,128)(2,1)S(1)} %collective-permute-done.16.refs_4_), channel_id=1, source_target_pairs={{0,4},{8,0},{16,8},{24,16},{28,24},{20,28},{12,20},{4,12},{1,5},{9... | collective-permute-start | bytes 393224 | tf_op jit(solution)/shard_map/ppermute | solution.py:385
  42.5 5.1 %collective-permute-start.19 = (bf16[144,512]{1,0:T(8,128)(2,1)S(1)}, bf16[144,512]{1,0:T(8,128)(2,1)S(1)}, u32[]{:S(2)}, u32[]{:S(2)}) collective-permute-start(bf16[144,512]{1,0:T(8,128)(2,1)S(1)} %collective-permute-done.18.refs_5_), channel_id=1, source_target_pairs={{0,8},{8,16},{16,24},{24,28},{28,20},{20,12},{12,4},{4,0},{1,9},{9... | collective-permute-start | bytes 442376 | tf_op jit(solution)/shard_map/ppermute | solution.py:385

commit v3 on v2

--- a/solution.py
+++ b/solution.py
@@ -149,13 +149,6 @@
     return counts.reshape(block_rows, block_rows)
 
 
-def own_counts_body(knn, own, out):
-    block_rows = out.shape[1]
-    for place in range(out.shape[0]):
-        counts = histogram(own[place], knn, block_rows)
-        out[place] = counts.astype(jnp.float32).astype(out.dtype)
-
-
 def split(weight):
     high = weight.astype(jnp.bfloat16)
     return high, (weight - high.astype(jnp.float32)).astype(jnp.bfloat16)
@@ -256,13 +249,35 @@
     pulls[1] = far if pulls_in is None else far + pulls_in[1]
 
 
+def present_row(entry):
+    return jnp.where(entry[0:1, :].astype(jnp.float32) <= float(entry.shape[1]), 1.0, 0.0)
+
+
 def tile_counts(own, entry, knn):
     back = histogram(entry, knn, own.shape[0]).astype(jnp.float32)
-    present = jnp.where(entry[0:1, :].astype(jnp.float32) <= float(own.shape[0]), 1.0, 0.0)
-    return transposed(own) + back, present
-
-
-def step_body(tiles, counted, first, constants, *refs):
+    return transposed(own) + back, present_row(entry)
+
+
+def forward_counts(entry, knn):
+    return histogram(entry, knn, entry.shape[1]).astype(jnp.float32).astype(jnp.bfloat16)
+
+
+def counts_body(tiles, pairs, knn, pad, *refs):
+    own, *notes, near, rest = refs
+    block_rows = near.shape[1]
+    for number, (place, spot) in enumerate(tiles):
+        entry = entry_of(notes, spot, pad, block_rows)
+        counts, _ = tile_counts(forward_counts(own[place], knn), entry, knn)
+        near[number] = counts.astype(near.dtype)
+    for number, (there, back) in enumerate(pairs):
+        forward = forward_counts(entry_of(notes, there, pad, block_rows), knn)
+        counts, _ = tile_counts(forward, entry_of(notes, back, pad, block_rows), knn)
+        near[len(tiles) + number] = counts.astype(near.dtype)
+    for number in range(rest.shape[0]):
+        rest[number] = forward_counts(own[len(tiles) + number], knn)
+
+
+def step_body(tiles, near, skipped, counted, first, constants, *refs):
     _, knn, pad = constants
     local_ref, note_ref, own_ref = refs[:3]
     kernel, weights = refs[-2:]
@@ -283,7 +298,10 @@
     for number, (place, pieces, front, spot) in enumerate(tiles):
         remote = rows_of(sources, pieces)
         entry = entry_of(sources, spot, pad, block_rows)
-        counts, present = tile_counts(own_ref[place], entry, knn)
+        if near is None:
+            counts, present = tile_counts(own_ref[place - skipped], entry, knn)
+        else:
+            counts, present = own_ref[near + number].astype(jnp.float32), present_row(entry)
         remote_norms = norm_parts(sources[front], knn, block_rows)
         kernel_phase(local, local_norms, remote, remote_norms, present, counts, constants, kernel, totals)
         before = held if number else held_in
@@ -293,11 +311,11 @@
         held[2][1] = totals[1]
 
 
-def sums_body(tiles, pairs, constants, *refs):
+def sums_body(tiles, pairs, near, near_pairs, constants, *refs):
     _, knn, pad = constants
     local_ref, note_ref, own_ref, base_ref, sums_in = refs[:5]
-    row_ref, kernels, all_counts = refs[-3:]
-    sources = refs[5:-3]
+    row_ref, kernels = refs[-2:]
+    sources = refs[5:-2]
     local = local_ref[...]
     block_rows = local.shape[0]
     local_norms = norm_parts(note_ref, knn, block_rows)
@@ -305,16 +323,14 @@
     for number, (place, pieces, front, spot) in enumerate(tiles):
         remote = rows_of(sources, pieces)
         entry = entry_of(sources, spot, pad, block_rows)
-        counts, present = tile_counts(own_ref[place], entry, knn)
-        all_counts[number] = counts.astype(all_counts.dtype)
+        counts, present = own_ref[near + number].astype(jnp.float32), present_row(entry)
         remote_norms = norm_parts(sources[front], knn, block_rows)
         kernel_phase(
             local, local_norms, remote, remote_norms, present, counts, constants, kernels.at[number], totals
         )
-    for left_pieces, left_front, right_pieces, right_front, there, back, weight in pairs:
-        entry = entry_of(sources, there, pad, block_rows)
-        forward = histogram(entry, knn, block_rows).astype(jnp.float32).astype(jnp.bfloat16)
-        counts, present = tile_counts(forward, entry_of(sources, back, pad, block_rows), knn)
+    for number, (left_pieces, left_front, right_pieces, right_front, _, back, weight) in enumerate(pairs):
+        counts = own_ref[near_pairs + number].astype(jnp.float32)
+        present = present_row(entry_of(sources, back, pad, block_rows))
         kernel_phase(
             rows_of(sources, left_pieces),
             norm_parts(sources[left_front], knn, block_rows),
@@ -332,14 +348,14 @@
     row_ref[...] = jnp.where(lane == 1, jnp.sum(totals[1]) * -0.5, row)
 
 
-def pull_body(tiles, *refs):
+def pull_body(tiles, near, *refs):
     kernels, counts = refs[:2]
     pulls_in, rows_in, pulls, row_sums, weights = refs[-5:]
     sources = refs[2:-5]
     for number, (_, pieces, _, _) in enumerate(tiles):
         before = (pulls, row_sums) if number else (pulls_in, rows_in)
         pull_phase(
-            rows_of(sources, pieces), kernels.at[number], counts.at[number], weights, *before, pulls, row_sums
+            rows_of(sources, pieces), kernels.at[number], counts.at[near + number], weights, *before, pulls, row_sums
         )
 
 
@@ -413,15 +429,6 @@
         name="prepare",
     )(*(pltpu.with_memory_space_constraint(x, pltpu.HBM) for x in (partners, pair_kind, neighbors, embeddings)))
     notes = both(right_note, left_note)
-    own_counts = pl.pallas_call(
-        functools.partial(own_counts_body, knn),
-        out_shape=jax.ShapeDtypeStruct((places, block_rows, block_rows), jnp.bfloat16),
-        in_specs=[VMEM],
-        out_specs=VMEM,
-        compiler_params=compiler_params(8),
-        cost_estimate=cost(1.0),
-        name="own_counts",
-    )(own)
     middle = block_rows // 2
     halves = [[block[:middle] for block in blocks], [block[middle:] for block in blocks]]
     arrived = {1: [blocks[0], blocks[1], *notes]}
@@ -429,10 +436,7 @@
         plain = both(*halves[0])
         other = both(*halves[1])
         halves = [plain, other]
-        notes = [
-            send(note[: height(step)], sign * step)
-            for note, sign in ((right_note, 1), (left_note, -1))
-        ]
+        notes = [send(note[: height(step)], sign * step) for note, sign in ((right_note, 1), (left_note, -1))]
         arrived[step] = plain + other + notes
     message = jax.ShapeDtypeStruct((middle + height(quarter + 1), features), embeddings.dtype)
     noted = pl.pallas_call(
@@ -500,7 +504,26 @@
         jax.ShapeDtypeStruct((2, block_rows, 1), jnp.float32),
         jax.ShapeDtypeStruct((2, 8, block_rows), jnp.float32),
     ]
+    near_tiles, near_pairs = [], []
+    for step in range(1, quarter + 1):
+        for side, sign in ((0, -1), (1, 1)):
+            _, row, column = spot_of(step, side, step)
+            near_tiles.append((place_of[sign * step], (2 * step - 2 + side, row, column)))
+    for distance in range(quarter + 1, half + 1):
+        lower = distance - quarter
+        there = (2 * lower - 2, *spot_of(lower, 0, distance)[1:])
+        near_pairs.append((there, (2 * quarter - 1, *spot_of(quarter, 1, distance)[1:])))
+    near_counts, own_counts = call(
+        functools.partial(counts_body, near_tiles, near_pairs, knn, pad),
+        [own] + [note for step in range(1, quarter + 1) for note in arrived[step][-2:]],
+        [
+            jax.ShapeDtypeStruct((len(near_tiles) + len(near_pairs), *square), jnp.bfloat16),
+            jax.ShapeDtypeStruct((places - len(near_tiles), *square), jnp.bfloat16),
+        ],
+        1.6,
+    )
     common = [local, right_note, own_counts]
+    nearby = [local, right_note, near_counts]
     state = None
     for step in range(1, half + 1):
         tiles = tiles_of(step)
@@ -523,19 +546,18 @@
                         factor,
                     )
                 )
-            window, kernels, counts = call(
-                functools.partial(sums_body, tiles, pairs, constants),
-                common + [base, state[2]] + sources,
+            window, kernels = call(
+                functools.partial(sums_body, tiles, pairs, 2 * step - 2, len(near_tiles), constants),
+                nearby + [base, state[2]] + sources,
                 [
                     jax.ShapeDtypeStruct((1, 128), jnp.float32),
                     jax.ShapeDtypeStruct((2, *square), jnp.float32),
-                    jax.ShapeDtypeStruct((2, *square), jnp.bfloat16),
                 ],
-                1.8,
+                1.2,
             )
-            operands = [kernels, counts] + arrived[step]
+            operands = [kernels, near_counts] + arrived[step]
             state = call(
-                functools.partial(pull_body, tiles),
+                functools.partial(pull_body, tiles, 2 * step - 2),
                 operands + list(state[:2]),
                 held[:2],
                 1.5,
@@ -544,12 +566,14 @@
             )
             continue
         counted = step < quarter
-        operands = common + arrived[step]
+        operands = (nearby if counted else common) + arrived[step]
         shapes = held if counted else held[:2]
         first = state is None
         aliases = {} if first else {len(operands) + k: k for k in range(len(shapes))}
         state = call(
-            functools.partial(step_body, tiles, counted, first, constants),
+            functools.partial(
+                step_body, tiles, 2 * step - 2 if counted else None, 2 * quarter, counted, first, constants
+            ),
             operands + ([] if first else list(state)),
             shapes,
             2.0,
@@ -596,6 +620,4 @@
 
 def solution(mesh):
     in_specs = (P(AXES, None), P(AXES, None), P(AXES, None), P(None, None, AXES))
-    return jax.shard_map(
-        column_step, mesh=mesh, in_specs=in_specs, out_specs=(P(AXES, None), P()), check_vma=False
-    )
+    return jax.shard_map(column_step, mesh=mesh, in_specs=in_specs, out_specs=(P(AXES, None), P()), check_vma=False)

time: 49.7 us -> 53.5 us (1.076)
  waiting for transfers between devices: 11.3 us -> 14.8 us
    ppermute x20, waiting for transfers between devices: 8.05 us -> 11.6 us  [send(): return lax.ppermute(value, 'wide', shift_pairs(groups, offset))]
    pallas_call x6 -> x7, Pallas kernels: 6.61 us -> 7.99 us  [call(): pl.pallas_call(body, out_shape=shapes, in_specs=[VMEM] * len(operands), o...]
    pallas_call x1 -> x0, Pallas kernels: 0.89 us -> none  [column_step(): pl.pallas_call(functools.partial(own_counts_body, knn), out_shape=jax.Sha...]
  transfers between devices with their start and end apart: 22 -> 22, of which waited for: 8 -> 10; matrix products, arithmetic and copies ran while one was open for 0% -> 0% of each run, Pallas kernels for 12% -> 14%
where the time goes in v3:
time: 53.5 us; the launch traced here: 53.4 us
  starting transfers between devices  28.4 us (53%)
  waiting for transfers between devices  14.8 us (28%)
  Pallas kernels  9.34 us (17%)
  between operations  0.77 us (1%)
    ppermute x20, starting transfers between devices, send(): return lax.ppermute(value, 'wide', shift_pairs(groups, offset))  26.8 us
    ppermute x20, waiting for transfers between devices, send(): return lax.ppermute(value, 'wide', shift_pairs(groups, offset))  11.6 us
    pallas_call x7, Pallas kernels, call(): pl.pallas_call(body, out_shape=shapes, in_specs=[VMEM] * len(operands), o...  7.99 us
    ppermute x2, waiting for transfers between devices, column_step(): lax.ppermute(window, 'narrow', [(k, k ^ bit) for k in range(columns)])  3.2 us
    ppermute x2, starting transfers between devices, column_step(): lax.ppermute(window, 'narrow', [(k, k ^ bit) for k in range(columns)])  1.59 us
    pallas_call x1, Pallas kernels, column_step(): pl.pallas_call(functools.partial(prepare_body, groups, offsets), out_shap...  1.33 us
  transfers between devices with their start and end apart: 22, of which 10 were waited for; matrix products, arithmetic and copies ran while one was open for 0% of the time, Pallas kernels for 14%

profile of v3, /device:TPU:0, one launch (start us, length us, event | category | flops | bytes accessed | tf_op | source)
XLA Modules:
  0.0 53.4 jit_solution(13090241652170156767)
XLA Ops:
  0.6 0.0 copy-start
  0.6 3.1 %collective-permute-start.4 = (bf16[256,512]{1,0:T(8,128)(2,1)}, bf16[256,512]{1,0:T(8,128)(2,1)S(1)}, u32[]{:S(2)}, u32[]{:S(2)}) collective-permute-start(bf16[256,512]{1,0:T(8,128)(2,1)} %refs_3_.1), channel_id=1, source_target_pairs={{0,8},{8,16},{16,24},{24,28},{28,20},{20,12},{12,4},{4,0},{1,9},{9... | collective-permute-start | bytes 786440 | tf_op jit(solution)/shard_map/ppermute | solution.py:401
  3.7 1.3 %prepare.1 = (bf16[32,512]{1,0:T(8,128)(2,1)S(1)}, bf16[32,512]{1,0:T(8,128)(2,1)S(1)}, bf16[7,16,256]{2,1,0:T(8,128)(2,1)S(1)}, f32[1,128]{1,0:T(1,128)S(1)}, bf16[256,512]{1,0:T(8,128)(2,1)S(1)}) custom-call(s32[1,7]{1,0:T(1,128)} %refs_0_.1, s32[1,7]{1,0:T(1,128)} %refs_1_.1, s32[7,15,256]{2,1,0:T(8,128)} %refs_2_.1, bf16[256,512]{1,0:T(8,128)(2,1)} %refs_3_.1), custom_call_target="tpu_custom_call" | custom-call | flops 1200000000 | bytes 3000000 | tf_op jit(solution)/shard_map/prepare/pallas_call | solution.py:410
  5.1 2.6 %collective-permute-start.2 = (bf16[32,512]{1,0:T(8,128)(2,1)S(1)}, bf16[32,512]{1,0:T(8,128)(2,1)S(1)}, u32[]{:S(2)}, u32[]{:S(2)}) collective-permute-start(bf16[32,512]{1,0:T(8,128)(2,1)S(1)} %get-tuple-element.25.refs_1_), channel_id=1, source_target_pairs={{0,16},{8,24},{16,28},{24,20},{28,12},{20,4},{12,0},{4,8},{1,17},{... | collective-permute-start | bytes 98312 | tf_op jit(solution)/shard_map/ppermute | solution.py:401
  7.7 1.5 %collective-permute-start = (bf16[32,512]{1,0:T(8,128)(2,1)S(1)}, bf16[32,512]{1,0:T(8,128)(2,1)S(1)}, u32[]{:S(2)}, u32[]{:S(2)}) collective-permute-start(bf16[32,512]{1,0:T(8,128)(2,1)S(1)} %get-tuple-element.25.refs_1_), channel_id=1, source_target_pairs={{0,8},{8,16},{16,24},{24,28},{28,20},{20,12},{12,4},{4,0},{1,9},{9... | collective-permute-start | bytes 98312 | tf_op jit(solution)/shard_map/ppermute | solution.py:401
  9.2 0.4 collective-permute-start.3
  9.6 0.4 collective-permute-start.1
  10.1 2.7 %collective-permute-done.2.refs_3_.refs_9_.right_lists.refs_6_ = bf16[32,512]{1,0:T(8,128)(2,1)S(1)} collective-permute-done((bf16[32,512]{1,0:T(8,128)(2,1)S(1)}, bf16[32,512]{1,0:T(8,128)(2,1)S(1)}, u32[]{:S(2)}, u32[]{:S(2)}) %collective-permute-start.2) | collective-permute-done | bytes 32800 | tf_op jit(solution)/shard_map/ppermute | solution.py:401
  12.8 0.0 copy-done
  12.8 1.6 %collective-permute-start.5 = (bf16[256,512]{1,0:T(8,128)(2,1)S(1)}, bf16[256,512]{1,0:T(8,128)(2,1)S(1)}, u32[]{:S(2)}, u32[]{:S(2)}) collective-permute-start(bf16[256,512]{1,0:T(8,128)(2,1)S(1)} %copy-done), channel_id=1, source_target_pairs={{0,4},{8,0},{16,8},{24,16},{28,24},{20,28},{12,20},{4,12},{1,5},{9... | collective-permute-start | bytes 786440 | tf_op jit(solution)/shard_map/ppermute | solution.py:401
  14.3 0.0 collective-permute-done.refs_1_.refs_5_.refs_13_
  14.3 0.4 collective-permute-done.3.refs_4_.refs_10_.left_lists.refs_7_
  14.7 0.0 collective-permute-done.1.refs_2_.refs_6_.refs_14_
  14.7 2.1 %shard_map.59 = (bf16[6,256,256]{2,1,0:T(8,128)(2,1)S(1)}, bf16[3,256,256]{2,1,0:T(8,128)(2,1)S(1)}) custom-call(bf16[7,16,256]{2,1,0:T(8,128)(2,1)S(1)} %get-tuple-element.26.refs_0_, bf16[32,512]{1,0:T(8,128)(2,1)S(1)} %collective-permute-done.refs_1_.refs_5_.refs_13_, bf16[32,512]{1,0:T(8,128)(2,1)S(1)} %collective-permute-done.1.refs_2_.refs_6_.refs_14_, ...), custom_call_target="tpu_custom_call" | custom-call | flops 1280000000 | bytes 3200000 | tf_op jit(solution)/shard_map/pallas_call | solution.py:485
  16.8 0.0 collective-permute-done.4.refs_3_.refs_11_
  16.8 1.3 %collective-permute-start.6 = (bf16[128,512]{1,0:T(8,128)(2,1)S(1)}, bf16[128,512]{1,0:T(8,128)(2,1)S(1)}, u32[]{:S(2)}, u32[]{:S(2)}) collective-permute-start(bf16[128,512]{1,0:T(8,128)(2,1)S(1)} %get-tuple-element.49), channel_id=1, source_target_pairs={{0,8},{8,16},{16,24},{24,28},{28,20},{20,12},{12,4},{4,0},{1,9},{9... | collective-permute-start | bytes 393224 | tf_op jit(solution)/shard_map/ppermute | solution.py:401
  18.2 1.4 %collective-permute-done.5.refs_4_.refs_12_ = bf16[256,512]{1,0:T(8,128)(2,1)S(1)} collective-permute-done((bf16[256,512]{1,0:T(8,128)(2,1)S(1)}, bf16[256,512]{1,0:T(8,128)(2,1)S(1)}, u32[]{:S(2)}, u32[]{:S(2)}) %collective-permute-start.5) | collective-permute-done | bytes 262176 | tf_op jit(solution)/shard_map/ppermute | solution.py:401
  19.5 1.7 %collective-permute-start.7 = (bf16[128,512]{1,0:T(8,128)(2,1)S(1)}, bf16[128,512]{1,0:T(8,128)(2,1)S(1)}, u32[]{:S(2)}, u32[]{:S(2)}) collective-permute-start(bf16[128,512]{1,0:T(8,128)(2,1)S(1)} %get-tuple-element.47), channel_id=1, source_target_pairs={{0,4},{8,0},{16,8},{24,16},{28,24},{20,28},{12,20},{4,12},{1,5},{9... | collective-permute-start | bytes 393224 | tf_op jit(solution)/shard_map/ppermute | solution.py:401
  21.3 0.3 collective-permute-start.8
  21.6 1.7 %collective-permute-start.9 = (bf16[128,512]{1,0:T(8,128)(2,1)S(1)}, bf16[128,512]{1,0:T(8,128)(2,1)S(1)}, u32[]{:S(2)}, u32[]{:S(2)}) collective-permute-start(bf16[128,512]{1,0:T(8,128)(2,1)S(1)} %get-tuple-element.46), channel_id=1, source_target_pairs={{0,4},{8,0},{16,8},{24,16},{28,24},{20,28},{12,20},{4,12},{1,5},{9... | collective-permute-start | bytes 393224 | tf_op jit(solution)/shard_map/ppermute | solution.py:401
  23.3 1.2 %shard_map.60 = (f32[2,256,512]{2,1,0:T(8,128)S(1)}, f32[2,256,1]{2,1,0:T(8,128)S(1)}, f32[2,8,256]{2,1,0:T(8,128)S(1)}) custom-call(bf16[256,512]{1,0:T(8,128)(2,1)S(1)} %get-tuple-element.24.refs_0_.refs_3_, bf16[32,512]{1,0:T(8,128)(2,1)S(1)} %get-tuple-element.25.refs_1_, bf16[6,256,256]{2,1,0:T(8,128)(2,1)S(1)} %get-tuple-element.28.refs_2_.refs_1_, ...), custom_call_target="tpu_custom_call" | custom-call | flops 1600000000 | bytes 4000000 | tf_op jit(solution)/shard_map/pallas_call | solution.py:485
  24.5 0.0 collective-permute-done.6.refs_5_.refs_2_
  24.5 0.0 collective-permute-done.7.refs_6_.refs_3_
  24.6 1.7 %collective-permute-done.8.refs_7_.right_block.refs_4_ = bf16[128,512]{1,0:T(8,128)(2,1)S(1)} collective-permute-done((bf16[128,512]{1,0:T(8,128)(2,1)S(1)}, bf16[128,512]{1,0:T(8,128)(2,1)S(1)}, u32[]{:S(2)}, u32[]{:S(2)}) %collective-permute-start.8) | collective-permute-done | bytes 131104 | tf_op jit(solution)/shard_map/ppermute | solution.py:401
  26.2 0.3 collective-permute-done.9.refs_8_.left_block.refs_5_
  26.6 0.9 %shard_map.61 = (f32[1,128]{1,0:T(1,128)S(1)}, f32[2,256,256]{2,1,0:T(8,128)S(1)}) custom-call(bf16[256,512]{1,0:T(8,128)(2,1)S(1)} %get-tuple-element.24.refs_0_.refs_3_, bf16[32,512]{1,0:T(8,128)(2,1)S(1)} %get-tuple-element.25.refs_1_, bf16[6,256,256]{2,1,0:T(8,128)(2,1)S(1)} %get-tuple-element.28.refs_2_.refs_1_, ...), custom_call_target="tpu_custom_call" | custom-call | flops 960000000 | bytes 2400000 | tf_op jit(solution)/shard_map/pallas_call | solution.py:485
  27.5 0.1 collective-permute-start.10
  27.6 1.1 %collective-permute-done.10 = f32[1,128]{1,0:T(1,128)S(1)} collective-permute-done((f32[1,128]{1,0:T(1,128)S(1)}, f32[1,128]{1,0:T(1,128)S(1)}, u32[]{:S(2)}, u32[]{:S(2)}) %collective-permute-start.10) | collective-permute-done | bytes 544 | tf_op jit(solution)/shard_map/ppermute | solution.py:586
  28.8 1.5 %collective-permute-start.11 = (f32[1,128]{1,0:T(1,128)S(1)}, f32[1,128]{1,0:T(1,128)S(1)}, u32[]{:S(2)}, u32[]{:S(2)}) collective-permute-start(f32[1,128]{1,0:T(1,128)S(1)} %add.6), channel_id=1, source_target_pairs={{0,2},{1,3},{2,0},{3,1},{4,6},{5,7},{6,4},{7,5},{8,10},{9,11},{10,... | collective-permute-start | bytes 1544 | tf_op jit(solution)/shard_map/ppermute | solution.py:586
  30.3 2.1 %collective-permute-done.11 = f32[1,128]{1,0:T(1,128)S(1)} collective-permute-done((f32[1,128]{1,0:T(1,128)S(1)}, f32[1,128]{1,0:T(1,128)S(1)}, u32[]{:S(2)}, u32[]{:S(2)}) %collective-permute-start.11) | collective-permute-done | bytes 544 | tf_op jit(solution)/shard_map/ppermute | solution.py:586
  32.3 0.9 %collective-permute-start.12 = (f32[1,128]{1,0:T(1,128)S(1)}, f32[1,128]{1,0:T(1,128)S(1)}, u32[]{:S(2)}, u32[]{:S(2)}) collective-permute-start(f32[1,128]{1,0:T(1,128)S(1)} %add.7), channel_id=1, source_target_pairs={{0,8},{8,16},{16,24},{24,28},{28,20},{20,12},{12,4},{4,0},{1,9},{9... | collective-permute-start | bytes 1544 | tf_op jit(solution)/shard_map/ppermute | solution.py:401
  33.2 1.6 %collective-permute-start.18 = (bf16[144,512]{1,0:T(8,128)(2,1)S(1)}, bf16[144,512]{1,0:T(8,128)(2,1)S(1)}, u32[]{:S(2)}, u32[]{:S(2)}) collective-permute-start(bf16[144,512]{1,0:T(8,128)(2,1)S(1)} %get-tuple-element.33), channel_id=1, source_target_pairs={{0,8},{8,16},{16,24},{24,28},{28,20},{20,12},{12,4},{4,0},{1,9},{9... | collective-permute-start | bytes 442376 | tf_op jit(solution)/shard_map/ppermute | solution.py:401
  34.8 0.5 collective-permute-start.21
  35.3 1.2 %collective-permute-start.16 = (bf16[128,512]{1,0:T(8,128)(2,1)S(1)}, bf16[128,512]{1,0:T(8,128)(2,1)S(1)}, u32[]{:S(2)}, u32[]{:S(2)}) collective-permute-start(bf16[128,512]{1,0:T(8,128)(2,1)S(1)} %collective-permute-done.7.refs_6_.refs_3_), channel_id=1, source_target_pairs={{0,4},{8,0},{16,8},{24,16},{28,24},{20,28},{12,20},{4,12},{1,5},{9... | collective-permute-start | bytes 393224 | tf_op jit(solution)/shard_map/ppermute | solution.py:401
  36.5 0.9 %collective-permute-start.20 = (bf16[128,512]{1,0:T(8,128)(2,1)S(1)}, bf16[128,512]{1,0:T(8,128)(2,1)S(1)}, u32[]{:S(2)}, u32[]{:S(2)}) collective-permute-start(bf16[128,512]{1,0:T(8,128)(2,1)S(1)} %collective-permute-done.6.refs_5_.refs_2_), channel_id=1, source_target_pairs={{0,8},{8,16},{16,24},{24,28},{28,20},{20,12},{12,4},{4,0},{1,9},{9... | collective-permute-start | bytes 393224 | tf_op jit(solution)/shard_map/ppermute | solution.py:401
  37.3 0.0 collective-permute-done.12
  37.3 1.2 %collective-permute-start.13 = (f32[1,128]{1,0:T(1,128)S(1)}, f32[1,128]{1,0:T(1,128)S(1)}, u32[]{:S(2)}, u32[]{:S(2)}) collective-permute-start(f32[1,128]{1,0:T(1,128)S(1)} %add.7), channel_id=1, source_target_pairs={{0,4},{8,0},{16,8},{24,16},{28,24},{20,28},{12,20},{4,12},{1,5},{9... | collective-permute-start | bytes 1544 | tf_op jit(solution)/shard_map/ppermute | solution.py:401
  38.5 0.6 %shard_map.62 = (f32[2,256,512]{2,1,0:T(8,128)S(1)}, f32[2,256,1]{2,1,0:T(8,128)S(1)}) custom-call(f32[2,256,256]{2,1,0:T(8,128)S(1)} %get-tuple-element.35.refs_0_, bf16[6,256,256]{2,1,0:T(8,128)(2,1)S(1)} %get-tuple-element.28.refs_2_.refs_1_, ...), custom_call_target="tpu_custom_call", output_to_operand_aliasing={{0}: (8, {}), {1}: (9, {})} | custom-call | flops 1200000000 | bytes 3000000 | tf_op jit(solution)/shard_map/pallas_call | solution.py:485
  39.1 3.0 %collective-permute-done.13 = f32[1,128]{1,0:T(1,128)S(1)} collective-permute-done((f32[1,128]{1,0:T(1,128)S(1)}, f32[1,128]{1,0:T(1,128)S(1)}, u32[]{:S(2)}, u32[]{:S(2)}) %collective-permute-start.13) | collective-permute-done | bytes 544 | tf_op jit(solution)/shard_map/ppermute | solution.py:401
  42.1 2.1 %collective-permute-start.14 = (f32[3,128]{1,0:T(4,128)S(1)}, f32[3,128]{1,0:T(4,128)S(1)}, u32[]{:S(2)}, u32[]{:S(2)}) collective-permute-start(f32[3,128]{1,0:T(4,128)S(1)} %pad_maximum_fusion.refs_0_), channel_id=1, source_target_pairs={{0,20},{8,12},{16,4},{24,0},{28,8},{20,16},{12,24},{4,28},{1,21},{... | collective-permute-start | bytes 4616 | tf_op jit(solution)/shard_map/ppermute | solution.py:401
  44.3 0.0 collective-permute-done.16.refs_4_
  44.3 1.8 %collective-permute-start.15 = (f32[3,128]{1,0:T(4,128)S(1)}, f32[3,128]{1,0:T(4,128)S(1)}, u32[]{:S(2)}, u32[]{:S(2)}) collective-permute-start(f32[3,128]{1,0:T(4,128)S(1)} %pad_maximum_fusion.refs_0_), channel_id=1, source_target_pairs={{0,24},{8,28},{16,20},{24,12},{28,4},{20,0},{12,8},{4,16},{1,25},{... | collective-permute-start | bytes 4616 | tf_op jit(solution)/shard_map/ppermute | solution.py:401
  46.0 0.0 collective-permute-done.20.refs_3_
  46.0 0.3 collective-permute-start.17
  46.3 0.0 collective-permute-done.18.refs_5_
  46.3 1.7 %collective-permute-start.19 = (bf16[144,512]{1,0:T(8,128)(2,1)S(1)}, bf16[144,512]{1,0:T(8,128)(2,1)S(1)}, u32[]{:S(2)}, u32[]{:S(2)}) collective-permute-start(bf16[144,512]{1,0:T(8,128)(2,1)S(1)} %collective-permute-done.18.refs_5_), channel_id=1, source_target_pairs={{0,8},{8,16},{16,24},{24,28},{28,20},{20,12},{12,4},{4,0},{1,9},{9... | collective-permute-start | bytes 442376 | tf_op jit(solution)/shard_map/ppermute | solution.py:401
  48.1 0.0 collective-permute-done.21.refs_6_
  48.1 1.3 %shard_map.63 = (f32[2,256,512]{2,1,0:T(8,128)S(1)}, f32[2,256,1]{2,1,0:T(8,128)S(1)}) custom-call(bf16[256,512]{1,0:T(8,128)(2,1)S(1)} %get-tuple-element.24.refs_0_.refs_3_, bf16[32,512]{1,0:T(8,128)(2,1)S(1)} %get-tuple-element.25.refs_1_, bf16[3,256,256]{2,1,0:T(8,128)(2,1)S(1)} %get-tuple-element.32.refs_2_, ...), custom_call_target="tpu_custom_call", output_to_operand_aliasing={{0}: (7, {}), {1}: (8, {})} | custom-call | flops 1600000000 | bytes 4000000 | tf_op jit(solution)/shard_map/pallas_call | solution.py:485
  49.3 1.7 %collective-permute-done.17.refs_3_ = bf16[128,512]{1,0:T(8,128)(2,1)S(1)} collective-permute-done((bf16[128,512]{1,0:T(8,128)(2,1)S(1)}, bf16[128,512]{1,0:T(8,128)(2,1)S(1)}, u32[]{:S(2)}, u32[]{:S(2)}) %collective-permute-start.17) | collective-permute-done | bytes 131104 | tf_op jit(solution)/shard_map/ppermute | solution.py:401
  51.0 0.5 collective-permute-done.19.refs_4_
  51.5 0.8 %shard_map.64 = (f32[2,256,512]{2,1,0:T(8,128)S(1)}, f32[2,256,1]{2,1,0:T(8,128)S(1)}) custom-call(bf16[256,512]{1,0:T(8,128)(2,1)S(1)} %get-tuple-element.24.refs_0_.refs_3_, bf16[32,512]{1,0:T(8,128)(2,1)S(1)} %get-tuple-element.25.refs_1_, bf16[3,256,256]{2,1,0:T(8,128)(2,1)S(1)} %get-tuple-element.32.refs_2_, ...), custom_call_target="tpu_custom_call", output_to_operand_aliasing={{0}: (5, {}), {1}: (6, {})} | custom-call | flops 1600000000 | bytes 4000000 | tf_op jit(solution)/shard_map/pallas_call | solution.py:485
  52.2 0.0 collective-permute-done.14.refs_1_
  52.3 0.0 collective-permute-done.15.refs_2_
  52.3 1.1 %shard_map.65 = (f32[256,512]{1,0:T(8,128)}, f32[1,1]{1,0:T(1,128)}) custom-call(f32[3,128]{1,0:T(4,128)S(1)} %pad_maximum_fusion.refs_0_, f32[3,128]{1,0:T(4,128)S(1)} %collective-permute-done.14.refs_1_, f32[3,128]{1,0:T(4,128)S(1)} %collective-permute-done.15.refs_2_, bf16[256,512]{1,0:T(8,128)(2,1)S(1)} %get-tuple-element.24.refs_0_.refs_3_, ...), custom_call_target="tpu_custom_call" | custom-call | flops 800000000 | bytes 2000000 | tf_op jit(solution)/shard_map/pallas_call | solution.py:485
  (6 shorter events, 0.1 us)
Async XLA Ops:
  0.6 12.1 %copy-start = (bf16[256,512]{1,0:T(8,128)(2,1)S(1)}, bf16[256,512]{1,0:T(8,128)(2,1)}, u32[]{:S(2)}) copy-start(bf16[256,512]{1,0:T(8,128)(2,1)} %refs_3_.1) | copy-start | bytes 786436
  0.6 16.2 %collective-permute-start.4 = (bf16[256,512]{1,0:T(8,128)(2,1)}, bf16[256,512]{1,0:T(8,128)(2,1)S(1)}, u32[]{:S(2)}, u32[]{:S(2)}) collective-permute-start(bf16[256,512]{1,0:T(8,128)(2,1)} %refs_3_.1), channel_id=1, source_target_pairs={{0,8},{8,16},{16,24},{24,28},{28,20},{20,12},{12,4},{4,0},{1,9},{9... | collective-permute-start | bytes 786440 | tf_op jit(solution)/shard_map/ppermute | solution.py:401
  5.1 7.7 %collective-permute-start.2 = (bf16[32,512]{1,0:T(8,128)(2,1)S(1)}, bf16[32,512]{1,0:T(8,128)(2,1)S(1)}, u32[]{:S(2)}, u32[]{:S(2)}) collective-permute-start(bf16[32,512]{1,0:T(8,128)(2,1)S(1)} %get-tuple-element.25.refs_1_), channel_id=1, source_target_pairs={{0,16},{8,24},{16,28},{24,20},{28,12},{20,4},{12,0},{4,8},{1,17},{... | collective-permute-start | bytes 98312 | tf_op jit(solution)/shard_map/ppermute | solution.py:401
  7.7 6.6 %collective-permute-start = (bf16[32,512]{1,0:T(8,128)(2,1)S(1)}, bf16[32,512]{1,0:T(8,128)(2,1)S(1)}, u32[]{:S(2)}, u32[]{:S(2)}) collective-permute-start(bf16[32,512]{1,0:T(8,128)(2,1)S(1)} %get-tuple-element.25.refs_1_), channel_id=1, source_target_pairs={{0,8},{8,16},{16,24},{24,28},{28,20},{20,12},{12,4},{4,0},{1,9},{9... | collective-permute-start | bytes 98312 | tf_op jit(solution)/shard_map/ppermute | solution.py:401
  9.2 5.5 %collective-permute-start.3 = (bf16[32,512]{1,0:T(8,128)(2,1)S(1)}, bf16[32,512]{1,0:T(8,128)(2,1)S(1)}, u32[]{:S(2)}, u32[]{:S(2)}) collective-permute-start(bf16[32,512]{1,0:T(8,128)(2,1)S(1)} %get-tuple-element.27), channel_id=1, source_target_pairs={{0,12},{8,4},{16,0},{24,8},{28,16},{20,24},{12,28},{4,20},{1,13},{... | collective-permute-start | bytes 98312 | tf_op jit(solution)/shard_map/ppermute | solution.py:401
  9.6 5.1 %collective-permute-start.1 = (bf16[32,512]{1,0:T(8,128)(2,1)S(1)}, bf16[32,512]{1,0:T(8,128)(2,1)S(1)}, u32[]{:S(2)}, u32[]{:S(2)}) collective-permute-start(bf16[32,512]{1,0:T(8,128)(2,1)S(1)} %get-tuple-element.27), channel_id=1, source_target_pairs={{0,4},{8,0},{16,8},{24,16},{28,24},{20,28},{12,20},{4,12},{1,5},{9... | collective-permute-start | bytes 98312 | tf_op jit(solution)/shard_map/ppermute | solution.py:401
  12.8 6.8 %collective-permute-start.5 = (bf16[256,512]{1,0:T(8,128)(2,1)S(1)}, bf16[256,512]{1,0:T(8,128)(2,1)S(1)}, u32[]{:S(2)}, u32[]{:S(2)}) collective-permute-start(bf16[256,512]{1,0:T(8,128)(2,1)S(1)} %copy-done), channel_id=1, source_target_pairs={{0,4},{8,0},{16,8},{24,16},{28,24},{20,28},{12,20},{4,12},{1,5},{9... | collective-permute-start | bytes 786440 | tf_op jit(solution)/shard_map/ppermute | solution.py:401
  16.8 7.7 %collective-permute-start.6 = (bf16[128,512]{1,0:T(8,128)(2,1)S(1)}, bf16[128,512]{1,0:T(8,128)(2,1)S(1)}, u32[]{:S(2)}, u32[]{:S(2)}) collective-permute-start(bf16[128,512]{1,0:T(8,128)(2,1)S(1)} %get-tuple-element.49), channel_id=1, source_target_pairs={{0,8},{8,16},{16,24},{24,28},{28,20},{20,12},{12,4},{4,0},{1,9},{9... | collective-permute-start | bytes 393224 | tf_op jit(solution)/shard_map/ppermute | solution.py:401
  19.5 5.0 %collective-permute-start.7 = (bf16[128,512]{1,0:T(8,128)(2,1)S(1)}, bf16[128,512]{1,0:T(8,128)(2,1)S(1)}, u32[]{:S(2)}, u32[]{:S(2)}) collective-permute-start(bf16[128,512]{1,0:T(8,128)(2,1)S(1)} %get-tuple-element.47), channel_id=1, source_target_pairs={{0,4},{8,0},{16,8},{24,16},{28,24},{20,28},{12,20},{4,12},{1,5},{9... | collective-permute-start | bytes 393224 | tf_op jit(solution)/shard_map/ppermute | solution.py:401
  21.3 5.0 %collective-permute-start.8 = (bf16[128,512]{1,0:T(8,128)(2,1)S(1)}, bf16[128,512]{1,0:T(8,128)(2,1)S(1)}, u32[]{:S(2)}, u32[]{:S(2)}) collective-permute-start(bf16[128,512]{1,0:T(8,128)(2,1)S(1)} %get-tuple-element.48), channel_id=1, source_target_pairs={{0,8},{8,16},{16,24},{24,28},{28,20},{20,12},{12,4},{4,0},{1,9},{9... | collective-permute-start | bytes 393224 | tf_op jit(solution)/shard_map/ppermute | solution.py:401
  21.6 5.0 %collective-permute-start.9 = (bf16[128,512]{1,0:T(8,128)(2,1)S(1)}, bf16[128,512]{1,0:T(8,128)(2,1)S(1)}, u32[]{:S(2)}, u32[]{:S(2)}) collective-permute-start(bf16[128,512]{1,0:T(8,128)(2,1)S(1)} %get-tuple-element.46), channel_id=1, source_target_pairs={{0,4},{8,0},{16,8},{24,16},{28,24},{20,28},{12,20},{4,12},{1,5},{9... | collective-permute-start | bytes 393224 | tf_op jit(solution)/shard_map/ppermute | solution.py:401
  27.5 1.2 %collective-permute-start.10 = (f32[1,128]{1,0:T(1,128)S(1)}, f32[1,128]{1,0:T(1,128)S(1)}, u32[]{:S(2)}, u32[]{:S(2)}) collective-permute-start(f32[1,128]{1,0:T(1,128)S(1)} %get-tuple-element.31), channel_id=1, source_target_pairs={{0,1},{1,0},{2,3},{3,2},{4,5},{5,4},{6,7},{7,6},{8,9},{9,8},{10,11... | collective-permute-start | bytes 1544 | tf_op jit(solution)/shard_map/ppermute | solution.py:586
  28.8 3.6 %collective-permute-start.11 = (f32[1,128]{1,0:T(1,128)S(1)}, f32[1,128]{1,0:T(1,128)S(1)}, u32[]{:S(2)}, u32[]{:S(2)}) collective-permute-start(f32[1,128]{1,0:T(1,128)S(1)} %add.6), channel_id=1, source_target_pairs={{0,2},{1,3},{2,0},{3,1},{4,6},{5,7},{6,4},{7,5},{8,10},{9,11},{10,... | collective-permute-start | bytes 1544 | tf_op jit(solution)/shard_map/ppermute | solution.py:586
  32.3 5.0 %collective-permute-start.12 = (f32[1,128]{1,0:T(1,128)S(1)}, f32[1,128]{1,0:T(1,128)S(1)}, u32[]{:S(2)}, u32[]{:S(2)}) collective-permute-start(f32[1,128]{1,0:T(1,128)S(1)} %add.7), channel_id=1, source_target_pairs={{0,8},{8,16},{16,24},{24,28},{28,20},{20,12},{12,4},{4,0},{1,9},{9... | collective-permute-start | bytes 1544 | tf_op jit(solution)/shard_map/ppermute | solution.py:401
  33.2 13.1 %collective-permute-start.18 = (bf16[144,512]{1,0:T(8,128)(2,1)S(1)}, bf16[144,512]{1,0:T(8,128)(2,1)S(1)}, u32[]{:S(2)}, u32[]{:S(2)}) collective-permute-start(bf16[144,512]{1,0:T(8,128)(2,1)S(1)} %get-tuple-element.33), channel_id=1, source_target_pairs={{0,8},{8,16},{16,24},{24,28},{28,20},{20,12},{12,4},{4,0},{1,9},{9... | collective-permute-start | bytes 442376 | tf_op jit(solution)/shard_map/ppermute | solution.py:401
  34.8 13.3 %collective-permute-start.21 = (bf16[144,512]{1,0:T(8,128)(2,1)S(1)}, bf16[144,512]{1,0:T(8,128)(2,1)S(1)}, u32[]{:S(2)}, u32[]{:S(2)}) collective-permute-start(bf16[144,512]{1,0:T(8,128)(2,1)S(1)} %get-tuple-element.34), channel_id=1, source_target_pairs={{0,4},{8,0},{16,8},{24,16},{28,24},{20,28},{12,20},{4,12},{1,5},{9... | collective-permute-start | bytes 442376 | tf_op jit(solution)/shard_map/ppermute | solution.py:401
  35.3 9.0 %collective-permute-start.16 = (bf16[128,512]{1,0:T(8,128)(2,1)S(1)}, bf16[128,512]{1,0:T(8,128)(2,1)S(1)}, u32[]{:S(2)}, u32[]{:S(2)}) collective-permute-start(bf16[128,512]{1,0:T(8,128)(2,1)S(1)} %collective-permute-done.7.refs_6_.refs_3_), channel_id=1, source_target_pairs={{0,4},{8,0},{16,8},{24,16},{28,24},{20,28},{12,20},{4,12},{1,5},{9... | collective-permute-start | bytes 393224 | tf_op jit(solution)/shard_map/ppermute | solution.py:401
  36.5 9.6 %collective-permute-start.20 = (bf16[128,512]{1,0:T(8,128)(2,1)S(1)}, bf16[128,512]{1,0:T(8,128)(2,1)S(1)}, u32[]{:S(2)}, u32[]{:S(2)}) collective-permute-start(bf16[128,512]{1,0:T(8,128)(2,1)S(1)} %collective-permute-done.6.refs_5_.refs_2_), channel_id=1, source_target_pairs={{0,8},{8,16},{16,24},{24,28},{28,20},{20,12},{12,4},{4,0},{1,9},{9... | collective-permute-start | bytes 393224 | tf_op jit(solution)/shard_map/ppermute | solution.py:401
  37.3 4.8 %collective-permute-start.13 = (f32[1,128]{1,0:T(1,128)S(1)}, f32[1,128]{1,0:T(1,128)S(1)}, u32[]{:S(2)}, u32[]{:S(2)}) collective-permute-start(f32[1,128]{1,0:T(1,128)S(1)} %add.7), channel_id=1, source_target_pairs={{0,4},{8,0},{16,8},{24,16},{28,24},{20,28},{12,20},{4,12},{1,5},{9... | collective-permute-start | bytes 1544 | tf_op jit(solution)/shard_map/ppermute | solution.py:401
  42.1 10.1 %collective-permute-start.14 = (f32[3,128]{1,0:T(4,128)S(1)}, f32[3,128]{1,0:T(4,128)S(1)}, u32[]{:S(2)}, u32[]{:S(2)}) collective-permute-start(f32[3,128]{1,0:T(4,128)S(1)} %pad_maximum_fusion.refs_0_), channel_id=1, source_target_pairs={{0,20},{8,12},{16,4},{24,0},{28,8},{20,16},{12,24},{4,28},{1,21},{... | collective-permute-start | bytes 4616 | tf_op jit(solution)/shard_map/ppermute | solution.py:401
  44.3 8.0 %collective-permute-start.15 = (f32[3,128]{1,0:T(4,128)S(1)}, f32[3,128]{1,0:T(4,128)S(1)}, u32[]{:S(2)}, u32[]{:S(2)}) collective-permute-start(f32[3,128]{1,0:T(4,128)S(1)} %pad_maximum_fusion.refs_0_), channel_id=1, source_target_pairs={{0,24},{8,28},{16,20},{24,12},{28,4},{20,0},{12,8},{4,16},{1,25},{... | collective-permute-start | bytes 4616 | tf_op jit(solution)/shard_map/ppermute | solution.py:401
  46.0 5.0 %collective-permute-start.17 = (bf16[128,512]{1,0:T(8,128)(2,1)S(1)}, bf16[128,512]{1,0:T(8,128)(2,1)S(1)}, u32[]{:S(2)}, u32[]{:S(2)}) collective-permute-start(bf16[128,512]{1,0:T(8,128)(2,1)S(1)} %collective-permute-done.16.refs_4_), channel_id=1, source_target_pairs={{0,4},{8,0},{16,8},{24,16},{28,24},{20,28},{12,20},{4,12},{1,5},{9... | collective-permute-start | bytes 393224 | tf_op jit(solution)/shard_map/ppermute | solution.py:401
  46.3 5.1 %collective-permute-start.19 = (bf16[144,512]{1,0:T(8,128)(2,1)S(1)}, bf16[144,512]{1,0:T(8,128)(2,1)S(1)}, u32[]{:S(2)}, u32[]{:S(2)}) collective-permute-start(bf16[144,512]{1,0:T(8,128)(2,1)S(1)} %collective-permute-done.18.refs_5_), channel_id=1, source_target_pairs={{0,8},{8,16},{16,24},{24,28},{28,20},{20,12},{12,4},{4,0},{1,9},{9... | collective-permute-start | bytes 442376 | tf_op jit(solution)/shard_map/ppermute | solution.py:401
